TPU v7x, 512 devices: a whole 4x4x16 slice. The times are simulated.
512 devices in a mesh: band: 128 (over z, x, core), chan: 4 (over y).
Axes of the slice: x: 4, y: 4, z: 16, core: 2. Of those that a mesh axis runs over, the one named last changes fastest.
Arguments:
- features: bfloat16 [384, 256, 128], P('chan', 'band'), may hold values from -6 to 6
- h_kernel: float32 [384, 47], P('chan'), may hold values from -0.875 to 0.875
- v_kernel: float32 [384, 47], P('chan'), may hold values from -0.875 to 0.875
- h_kernel_avg: float32 [384, 47], P('chan'), may hold values from -0.875 to 0.875
- v_kernel_avg: float32 [384, 47], P('chan'), may hold values from -0.875 to 0.875
- norm_gain: float32 [384], replicated, may hold values from 0.1 to 1.9
- w_in: bfloat16 [384, 1536], replicated, may hold values from -0.3125 to 0.3125
- w_out: bfloat16 [1536, 384], replicated, may hold values from -0.15625 to 0.15625
- cotangent: bfloat16 [384, 256, 128], P('chan', 'band'), may hold values from -6 to 6
- tissue: int32 [256, 128], P('band'), may hold values 0 or 1
Outputs:
- block_out: bfloat16 [384, 256, 128], P('chan', 'band')
- h_kernel_new: float32 [384, 47], P('chan')
- v_kernel_new: float32 [384, 47], P('chan')
- h_kernel_swa: float32 [384, 47], P('chan')
- v_kernel_swa: float32 [384, 47], P('chan')
All inputs are finite; a program needn't handle non-finite values. No bound on the sum of `tissue` on one device may be relied on, other than what follows from the above.
Results may differ from a plain program's by a relative error of at most 0.0063.
Values may be sent and summed in bfloat16 or wider, within the bound.
A program may use at most 64 MiB of HBM per device.

v0:
```python
import math

import jax
import jax.numpy as jnp
from jax import lax
from jax.sharding import PartitionSpec as P

AVERAGED = 4


EPSILON = 1e-06
STEP_SIZE = 0.1
ROOT_HALF = math.sqrt(0.5)
INV_ROOT_TWO_PI = 1.0 / math.sqrt(2.0 * math.pi)


def along_last(source, kernel):
    radius = (kernel.shape[1] - 1) // 2
    return lax.conv_general_dilated(
        source[None],
        kernel[:, None, None, :],
        (1, 1),
        ((0, 0), (radius, radius)),
        dimension_numbers=("NCHW", "OIHW", "NCHW"),
        feature_group_count=kernel.shape[0],
        preferred_element_type=jnp.float32,
    )[0]


def kernel_grad(source, upstream, radius):
    result = lax.conv_general_dilated(
        source[None],
        upstream[:, None],
        (1, 1),
        ((0, 0), (radius, radius)),
        dimension_numbers=("NCHW", "OIHW", "NCHW"),
        feature_group_count=source.shape[0],
        preferred_element_type=jnp.float32,
    )
    return result.reshape(source.shape[0], 2 * radius + 1)


def pointwise(values, upstream, norm_gain, w_in, w_out):
    widened = values.astype(jnp.float32)
    centred = widened - jnp.mean(widened, axis=0, keepdims=True)
    inverse = lax.rsqrt(jnp.mean(centred * centred, axis=0, keepdims=True) + EPSILON)
    standard = centred * inverse
    normed = (standard * norm_gain[:, None]).astype(jnp.bfloat16)
    preact = jnp.dot(w_in.T, normed, preferred_element_type=jnp.float32)
    cumulative = 0.5 * (1.0 + lax.erf(preact * ROOT_HALF))
    activated = (preact * cumulative).astype(jnp.bfloat16)
    branch = jnp.dot(w_out.T, activated, preferred_element_type=jnp.float32).astype(jnp.bfloat16)
    grad_act = jnp.dot(w_out, upstream, preferred_element_type=jnp.float32)
    density = jnp.exp(-0.5 * preact * preact) * INV_ROOT_TWO_PI
    grad_pre = (grad_act * (cumulative + preact * density)).astype(jnp.bfloat16)
    grad_normed = jnp.dot(w_in, grad_pre, preferred_element_type=jnp.float32)
    scaled = grad_normed * norm_gain[:, None]
    grad_values = (
        scaled
        - jnp.mean(scaled, axis=0, keepdims=True)
        - standard * jnp.mean(scaled * standard, axis=0, keepdims=True)
    ) * inverse
    return (branch, grad_values.astype(jnp.bfloat16))


def local(
    features,
    h_kernel,
    v_kernel,
    h_kernel_avg,
    v_kernel_avg,
    norm_gain,
    w_in,
    w_out,
    cotangent,
    tissue,
):
    band_count = lax.axis_size("band")
    channels, row_count, map_width = features.shape
    columns = map_width // band_count
    height = row_count * band_count
    radius = (h_kernel.shape[1] - 1) // 2
    h_half = h_kernel.astype(jnp.bfloat16)
    v_half = v_kernel.astype(jnp.bfloat16)
    smoothed = along_last(features, h_half).astype(jnp.bfloat16)
    weighted = cotangent * tissue.astype(jnp.bfloat16)[None]

    def split_rows(source):
        return source.reshape(channels, row_count, band_count, columns)

    def finish_columns(source):
        return jnp.swapaxes(source.reshape(channels, height, columns), 1, 2)

    def split_columns(source):
        return source.reshape(channels, columns, band_count, row_count)

    def finish_rows(source):
        return jnp.swapaxes(source.reshape(channels, map_width, row_count), 1, 2)

    smooth_cols = finish_columns(
        lax.all_to_all(split_rows(smoothed), "band", split_axis=2, concat_axis=1, tiled=True)
    )
    mixed_cols = along_last(smooth_cols, v_half).astype(jnp.bfloat16)
    mixed_rows = finish_rows(
        lax.all_to_all(split_columns(mixed_cols), "band", split_axis=2, concat_axis=1, tiled=True)
    )
    layout_shape = mixed_rows.shape
    cell_values, cell_grads = (
        lax.all_to_all(
            mixed_rows.reshape(channels, -1), "chan", split_axis=1, concat_axis=0, tiled=True
        ),
        lax.all_to_all(
            weighted.reshape(channels, -1), "chan", split_axis=1, concat_axis=0, tiled=True
        ),
    )
    branch, grad_mixed = pointwise(cell_values, cell_grads, norm_gain, w_in, w_out)
    branch, grad_mixed = (
        lax.all_to_all(branch, "chan", split_axis=0, concat_axis=1, tiled=True),
        lax.all_to_all(grad_mixed, "chan", split_axis=0, concat_axis=1, tiled=True),
    )
    branch = branch.reshape(layout_shape)
    grad_mixed = grad_mixed.reshape(layout_shape)
    grad_cols = finish_columns(
        lax.all_to_all(split_rows(grad_mixed), "band", split_axis=2, concat_axis=1, tiled=True)
    )
    block_out = (features.astype(jnp.float32) + branch.astype(jnp.float32)).astype(jnp.bfloat16)
    v_grad = kernel_grad(smooth_cols, grad_cols, radius)
    back_cols = along_last(grad_cols, v_half[:, ::-1]).astype(jnp.bfloat16)
    back_rows = finish_rows(
        lax.all_to_all(split_columns(back_cols), "band", split_axis=2, concat_axis=1, tiled=True)
    )
    h_grad = kernel_grad(features, back_rows, radius)
    h_grad, v_grad = lax.psum((h_grad, v_grad), "band")
    squares = (jnp.sum(h_grad * h_grad, axis=1) + jnp.sum(v_grad * v_grad, axis=1)) / (
        2 * h_kernel.shape[1]
    )
    inverse_rms = lax.rsqrt(squares + EPSILON)[:, None]
    h_new = h_kernel - STEP_SIZE * h_grad * inverse_rms
    v_new = v_kernel - STEP_SIZE * v_grad * inverse_rms
    h_swa = (AVERAGED * h_kernel_avg + h_new) / (AVERAGED + 1)
    v_swa = (AVERAGED * v_kernel_avg + v_new) / (AVERAGED + 1)
    return (block_out, h_new, v_new, h_swa, v_swa)


def solution(mesh):
    return jax.shard_map(
        local,
        mesh=mesh,
        in_specs=(
            P("chan", "band", None),
            P("chan", None),
            P("chan", None),
            P("chan", None),
            P("chan", None),
            P(),
            P(),
            P(),
            P("chan", "band", None),
            P("band", None),
        ),
        out_specs=(
            P("chan", "band", None),
            P("chan", None),
            P("chan", None),
            P("chan", None),
            P("chan", None),
        ),
        check_vma=False,
    )
```

profile of v0, /device:TPU:1, one launch (start us, length us, event | category | flops | bytes accessed | tf_op | source)
XLA Modules:
  0.0 636.0 jit_solution(4888669624352745489)
XLA Ops:
  0.6 1.1 copy.96
  1.7 0.7 convert_bitcast_fusion.1
  2.5 0.9 convolution_convert_fusion.2
  3.5 0.8 copy.99
  4.3 20.4 %all-to-all-start = ((bf16[96,2,128,1]{0,1,3,2:T(2,128)(2,1)}), bf16[96,2,128,1]{0,1,3,2:T(2,128)(2,1)S(1)}, u32[]{:S(2)}, u32[]{:S(2)}) async-start(bf16[96,2,128,1]{0,1,3,2:T(2,128)(2,1)} %copy.99), calls=%async_computation | async-start | bytes 131072 | tf_op jit(solution)/shard_map/all_to_all | solution.py:101
  24.9 14.7 %all-to-all-done = bf16[96,2,128,1]{0,1,3,2:T(2,128)(2,1)S(1)} async-done(((bf16[96,2,128,1]{0,1,3,2:T(2,128)(2,1)}), bf16[96,2,128,1]{0,1,3,2:T(2,128)(2,1)S(1)}, u32[]{:S(2)}, u32[]{:S(2)}) %all-to-all-start) | async-done | bytes 49184 | tf_op jit(solution)/shard_map/all_to_all | solution.py:101
  39.8 2.1 convolution_convert_fusion.1
  42.6 5.6 all-to-all-start.1
  48.9 14.4 %all-to-all-done.1 = bf16[96,1,128,2]{0,3,1,2:T(2,128)(2,1)S(1)} async-done(((bf16[96,1,128,2]{0,3,1,2:T(2,128)(2,1)}), bf16[96,1,128,2]{0,3,1,2:T(2,128)(2,1)S(1)}, u32[]{:S(2)}, u32[]{:S(2)}) %all-to-all-start.1) | async-done | bytes 49184 | tf_op jit(solution)/shard_map/all_to_all | solution.py:105
  63.3 4.2 all-to-all-start.4
  68.1 3.8 all-to-all-done.4
  72.0 3.3 all-to-all-start.2
  75.4 4.3 all-to-all-done.2
  81.3 0.9 fusion.22
  83.2 3.3 all-to-all-start.5
  87.6 3.4 all-to-all-done.5
  91.0 3.3 all-to-all-start.3
  95.1 3.6 all-to-all-done.3
  98.7 10.4 %all-to-all-start.6 = ((bf16[96,2,128,1]{0,1,3,2:T(2,128)(2,1)}), bf16[96,2,128,1]{0,1,3,2:T(2,128)(2,1)S(1)}, u32[]{:S(2)}, u32[]{:S(2)}) async-start(bf16[96,2,128,1]{0,1,3,2:T(2,128)(2,1)} %copy.111), calls=%async_computation.6 | async-start | bytes 131072 | tf_op jit(solution)/shard_map/all_to_all | solution.py:124
  109.9 14.3 %all-to-all-done.6 = bf16[96,2,128,1]{0,1,3,2:T(2,128)(2,1)S(1)} async-done(((bf16[96,2,128,1]{0,1,3,2:T(2,128)(2,1)}), bf16[96,2,128,1]{0,1,3,2:T(2,128)(2,1)S(1)}, u32[]{:S(2)}, u32[]{:S(2)}) %all-to-all-start.6) | async-done | bytes 49184 | tf_op jit(solution)/shard_map/all_to_all | solution.py:124
  124.2 2.1 convolution_convert_fusion
  126.9 5.7 all-to-all-start.7
  133.3 14.4 %all-to-all-done.7 = bf16[96,1,128,2]{0,3,1,2:T(2,128)(2,1)S(1)} async-done(((bf16[96,1,128,2]{0,3,1,2:T(2,128)(2,1)}), bf16[96,1,128,2]{0,3,1,2:T(2,128)(2,1)S(1)}, u32[]{:S(2)}, u32[]{:S(2)}) %all-to-all-start.7) | async-done | bytes 49184 | tf_op jit(solution)/shard_map/all_to_all | solution.py:130
  148.8 486.5 %all-reduce = (f32[96,47]{0,1:T(8,128)S(1)}, f32[96,47]{0,1:T(8,128)S(1)}) all-reduce(f32[96,47]{0,1:T(8,128)S(1)} %bitcast.101, f32[96,47]{0,1:T(8,128)S(1)} %bitcast.100), channel_id=1, replica_groups=mesh['band'=128,'chan'=4] {'band'}, use_global_device_ids=true, to_apply=%region_4.0 | all-reduce | flops 9024 | bytes 72192 | tf_op jit(solution)/shard_map/psum | solution.py:133
  (65 shorter events, 10.8 us)
Async XLA Ops:
  0.6 79.6 %copy-start = (bf16[384,1536]{1,0:T(8,128)(2,1)S(1)}, bf16[384,1536]{1,0:T(8,128)(2,1)}, u32[]{:S(2)}) copy-start(bf16[384,1536]{1,0:T(8,128)(2,1)} %param.16) | copy-start | bytes 3538948
  2.5 22.2 %copy-start.5 = (bf16[96,2,128]{2,1,0:T(2,128)(2,1)S(1)}, bf16[96,2,128]{2,1,0:T(2,128)(2,1)}, u32[]{:S(2)}) copy-start(bf16[96,2,128]{2,1,0:T(2,128)(2,1)} %param.18) | copy-start | bytes 147460
  2.5 22.4 %copy-start.9 = (s32[2,128]{1,0:T(2,128)S(1)}, s32[2,128]{1,0:T(2,128)}, u32[]{:S(2)}) copy-start(s32[2,128]{1,0:T(2,128)} %param.19) | copy-start | bytes 3076
  2.5 22.4 %copy-start.2 = (f32[96,47]{0,1:T(8,128)S(1)}, f32[96,47]{0,1:T(8,128)}, u32[]{:S(2)}) copy-start(f32[96,47]{0,1:T(8,128)} %param.12) | copy-start | bytes 54148
  4.3 35.3 %all-to-all-start = ((bf16[96,2,128,1]{0,1,3,2:T(2,128)(2,1)}), bf16[96,2,128,1]{0,1,3,2:T(2,128)(2,1)S(1)}, u32[]{:S(2)}, u32[]{:S(2)}) async-start(bf16[96,2,128,1]{0,1,3,2:T(2,128)(2,1)} %copy.99), calls=%async_computation | async-start | bytes 131072 | tf_op jit(solution)/shard_map/all_to_all | solution.py:101
  41.9 38.3 %copy-start.8 = (f32[384]{0:T(512)S(1)}, f32[384]{0:T(512)}, u32[]{:S(2)}) copy-start(f32[384]{0:T(512)} %param.15) | copy-start | bytes 4612
  42.6 20.7 %all-to-all-start.1 = ((bf16[96,1,128,2]{0,3,1,2:T(2,128)(2,1)}), bf16[96,1,128,2]{0,3,1,2:T(2,128)(2,1)S(1)}, u32[]{:S(2)}, u32[]{:S(2)}) async-start(bf16[96,1,128,2]{0,3,1,2:T(2,128)(2,1)} %bitcast.7), calls=%async_computation.1 | async-start | bytes 131072 | tf_op jit(solution)/shard_map/all_to_all | solution.py:105
  63.3 8.7 %all-to-all-start.4 = ((bf16[96,4,64]{0,2,1:T(8,128)(2,1)}), bf16[96,4,64]{0,2,1:T(8,128)(2,1)S(1)}, u32[]{:S(2)}, u32[]{:S(2)}) async-start(bf16[96,4,64]{0,2,1:T(8,128)(2,1)} %bitcast.16), calls=%async_computation.4 | async-start | bytes 131072 | tf_op jit(solution)/shard_map/all_to_all | solution.py:112
  72.0 7.7 %all-to-all-start.2 = ((bf16[96,4,64]{0,2,1:T(8,128)(2,1)}), bf16[96,4,64]{0,2,1:T(8,128)(2,1)S(1)}, u32[]{:S(2)}, u32[]{:S(2)}) async-start(bf16[96,4,64]{0,2,1:T(8,128)(2,1)} %bitcast.10), calls=%async_computation.2 | async-start | bytes 131072 | tf_op jit(solution)/shard_map/all_to_all | solution.py:109
  80.0 1.3 copy-start.1
  82.5 11.8 %copy-start.3 = (bf16[96,2,128]{2,1,0:T(2,128)(2,1)S(1)}, bf16[96,2,128]{2,1,0:T(2,128)(2,1)}, u32[]{:S(2)}) copy-start(bf16[96,2,128]{2,1,0:T(2,128)(2,1)} %param.10) | copy-start | bytes 147460
  83.2 7.7 %all-to-all-start.5 = ((bf16[4,96,64]{1,2,0:T(8,128)(2,1)}), bf16[4,96,64]{1,2,0:T(8,128)(2,1)S(1)}, u32[]{:S(2)}, u32[]{:S(2)}) async-start(bf16[4,96,64]{1,2,0:T(8,128)(2,1)} %copy.110), calls=%async_computation.5 | async-start | bytes 131072 | tf_op jit(solution)/shard_map/all_to_all | solution.py:119
  91.0 7.7 %all-to-all-start.3 = ((bf16[4,96,64]{1,2,0:T(8,128)(2,1)}), bf16[4,96,64]{1,2,0:T(8,128)(2,1)S(1)}, u32[]{:S(2)}, u32[]{:S(2)}) async-start(bf16[4,96,64]{1,2,0:T(8,128)(2,1)} %copy.107), calls=%async_computation.3 | async-start | bytes 131072 | tf_op jit(solution)/shard_map/all_to_all | solution.py:118
  98.7 25.5 %all-to-all-start.6 = ((bf16[96,2,128,1]{0,1,3,2:T(2,128)(2,1)}), bf16[96,2,128,1]{0,1,3,2:T(2,128)(2,1)S(1)}, u32[]{:S(2)}, u32[]{:S(2)}) async-start(bf16[96,2,128,1]{0,1,3,2:T(2,128)(2,1)} %copy.111), calls=%async_computation.6 | async-start | bytes 131072 | tf_op jit(solution)/shard_map/all_to_all | solution.py:124
  126.9 20.8 %all-to-all-start.7 = ((bf16[96,1,128,2]{0,3,1,2:T(2,128)(2,1)}), bf16[96,1,128,2]{0,3,1,2:T(2,128)(2,1)S(1)}, u32[]{:S(2)}, u32[]{:S(2)}) async-start(bf16[96,1,128,2]{0,3,1,2:T(2,128)(2,1)} %bitcast.26), calls=%async_computation.7 | async-start | bytes 131072 | tf_op jit(solution)/shard_map/all_to_all | solution.py:130
  148.0 487.3 %copy-start.4 = (f32[96,47]{0,1:T(8,128)S(1)}, f32[96,47]{0,1:T(8,128)}, u32[]{:S(2)}) copy-start(f32[96,47]{0,1:T(8,128)} %param.11) | copy-start | bytes 54148
  148.0 487.3 %copy-start.6 = (f32[96,47]{0,1:T(8,128)S(1)}, f32[96,47]{0,1:T(8,128)}, u32[]{:S(2)}) copy-start(f32[96,47]{0,1:T(8,128)} %param.14) | copy-start | bytes 54148
  148.0 487.3 %copy-start.7 = (f32[96,47]{0,1:T(8,128)S(1)}, f32[96,47]{0,1:T(8,128)}, u32[]{:S(2)}) copy-start(f32[96,47]{0,1:T(8,128)} %param.13) | copy-start | bytes 54148
where the time goes:
time: 640 us; the launch traced here: 636 us
  blocking collectives  487 us (76%)
  waiting for transfers between devices  72.9 us (11%)
  starting transfers between devices  56.2 us (9%)
  local copies, waits for them, and re-layouts  8.5 us (1%)
  matrix products  8.12 us (1%)
    psum x1, blocking collectives, local(): h_grad, v_grad = lax.psum((h_grad, v_grad), 'band')  487 us
    all_to_all x1, starting transfers between devices, local(): lax.all_to_all(split_rows(smoothed), 'band', split_axis=2, concat_axis=1,...  20.4 us
    all_to_all x1, waiting for transfers between devices, local(): lax.all_to_all(split_rows(smoothed), 'band', split_axis=2, concat_axis=1,...  14.7 us
    all_to_all x1, waiting for transfers between devices, local(): lax.all_to_all(split_columns(back_cols), 'band', split_axis=2, concat_axi...  14.4 us
    all_to_all x1, waiting for transfers between devices, local(): lax.all_to_all(split_columns(mixed_cols), 'band', split_axis=2, concat_ax...  14.4 us
    all_to_all x1, waiting for transfers between devices, local(): lax.all_to_all(split_rows(grad_mixed), 'band', split_axis=2, concat_axis=...  14.3 us
  transfers between devices with their start and end apart: 8, of which 8 were waited for; matrix products, arithmetic and copies ran while one was open for 1% of the time, Pallas kernels for 0%

commit v1 on v0

v1 whole, which is shorter than its diff:
```python
import math

import jax
import jax.numpy as jnp
from jax import lax
from jax.experimental import pallas as pl
from jax.experimental.pallas import tpu as pltpu
from jax.sharding import PartitionSpec as P

AVERAGED = 4
EPSILON = 1e-06
STEP_SIZE = 0.1
ROOT_HALF = math.sqrt(0.5)
INV_ROOT_TWO_PI = 1.0 / math.sqrt(2.0 * math.pi)

MESH = pl.DeviceIdType.MESH
BF16 = jnp.bfloat16
F32 = jnp.float32

PLACES = 8
LEVELS = 16
COUNT_Y = 4
ROWS = 2 * PLACES
GROUPS = 6
GROUP = 16
LOCAL = GROUPS * GROUP
C = COUNT_Y * LOCAL
HID = 1536
K = 47
RADIUS = 23
W = 128
HALO = 24
TALL = ROWS + 2 * HALO
BLOCK = 256


def wait_bytes(view, sem):
    pltpu.make_async_copy(view, view, sem).wait()


def kernel(
    f_ref,
    w_ref,
    h_ref,
    v_ref,
    gain_ref,
    w_in_hbm,
    w_out_hbm,
    out_ref,
    up_ref,
    w_in,
    w_out,
    w_in_t,
    w_out_t,
    gain,
    taps,
    smoothed,
    tall_s,
    tall_f,
    wide_s,
    wide_f,
    v_taps,
    shifted,
    mixed,
    cell_grads,
    grad_act,
    cell_values,
    standard,
    inverse_rows,
    normed,
    activated,
    grad_pre,
    grad_cells,
    grad_rows,
    branch_cells,
    branch_rows,
    partial,
    partials,
    update,
    updates,
    load_sem,
    here_sem,
    rows_send,
    rows_recv,
    halo_send,
    halo_recv,
    cot_send,
    cot_recv,
    mix_send,
    mix_recv,
    back_send,
    back_recv,
    branch_send,
    branch_recv,
    sum_send,
    sum_recv,
    all_send,
    all_recv,
):
    band = lax.axis_index("band")
    y = lax.axis_index("chan")
    z = band // PLACES
    place = band % PLACES
    core = band % 2
    works = place < GROUPS
    idles = place >= GROUPS
    points = core == y // 2
    rests = core != y // 2
    my_row = 2 * place + y % 2
    level = z * PLACES

    def remote(src, dst, send, recv, to_band, to_y):
        return pltpu.make_async_remote_copy(
            src_ref=src,
            dst_ref=dst,
            send_sem=send,
            recv_sem=recv,
            device_id=(to_band, to_y),
            device_id_type=MESH,
        )

    def go(stays, src, dst, send, recv, here, to_band, to_y):
        @pl.when(stays)
        def _():
            pltpu.make_async_copy(src, dst, here).start()

        @pl.when(jnp.logical_not(stays))
        def _():
            remote(src, dst, send, recv, to_band, to_y).start()

    def loop(count):
        return lambda body: lax.fori_loop(0, count, lambda i, c: (body(i), c)[1], 0)

    barrier = pltpu.get_barrier_semaphore()

    @loop(PLACES * COUNT_Y)
    def _(i):
        to_place = i // COUNT_Y
        to_y = i % COUNT_Y

        @pl.when(jnp.logical_or(to_place != place, to_y != y))
        def _():
            pl.semaphore_signal(
                barrier, 1, device_id=(level + to_place, to_y), device_id_type=MESH
            )

    @loop(LEVELS)
    def _(i):
        @pl.when(jnp.logical_and(works, i != z))
        def _():
            pl.semaphore_signal(
                barrier, 1, device_id=(i * PLACES + place, y), device_id_type=MESH
            )

    load_in = pltpu.make_async_copy(w_in_hbm, w_in, load_sem.at[0])
    load_out = pltpu.make_async_copy(w_out_hbm, w_out, load_sem.at[1])
    load_in.start()
    load_out.start()

    taps[...] = jnp.zeros((2, W, W), F32)
    taps[0, 0:K, 0:LOCAL] = h_ref[...]
    taps[1, 0:K, 0:LOCAL] = v_ref[...]
    h_half = taps[0].T[0:LOCAL].astype(BF16).astype(F32)
    taps[1] = taps[1].T.astype(BF16).astype(F32)
    column = lax.broadcasted_iota(jnp.int32, (LOCAL, W), 1)
    sources = [f_ref[:, row].reshape(LOCAL, W).astype(F32) for row in range(2)]
    sums = [jnp.zeros((LOCAL, W), F32) for row in range(2)]
    for t in range(K):
        weight = jnp.broadcast_to(h_half[:, t : t + 1], (LOCAL, W))
        if t < RADIUS:
            weight = jnp.where(column >= RADIUS - t, weight, 0.0)
        if t > RADIUS:
            weight = jnp.where(column < W + RADIUS - t, weight, 0.0)
        for row in range(2):
            moved = sources[row]
            if t != RADIUS:
                moved = pltpu.roll(moved, (RADIUS - t) % W, 1)
            sums[row] = sums[row] + weight * moved
    for row in range(2):
        smoothed[:, row] = sums[row].astype(BF16).reshape(GROUPS, GROUP, W)

    @pl.when(works)
    def _():
        pl.semaphore_wait(barrier, PLACES * COUNT_Y - 1 + LEVELS - 1)

    @pl.when(idles)
    def _():
        pl.semaphore_wait(barrier, PLACES * COUNT_Y - 1)

    own_pair = pl.ds(HALO + 2 * place, 2)

    @loop(GROUPS)
    def _(g):
        go(
            g == place,
            smoothed.at[g],
            tall_s.at[own_pair],
            rows_send.at[0],
            rows_recv.at[0],
            here_sem.at[0],
            level + g,
            y,
        )

    for row in range(2):
        go(
            jnp.logical_and(points, y % 2 == row),
            w_ref.at[row],
            cell_grads.at[y],
            cot_send,
            cot_recv,
            here_sem.at[1],
            band,
            2 * core + row,
        )

    @loop(GROUPS)
    def _(g):
        go(
            g == place,
            f_ref.at[g],
            tall_f.at[own_pair],
            rows_send.at[1],
            rows_recv.at[1],
            here_sem.at[2],
            level + g,
            y,
        )

    moves = (
        (1, HALO, 8, ROWS),
        (-1, HALO, HALO + ROWS, ROWS),
        (2, HALO + 8, 0, 8),
        (-2, HALO, HALO + 2 * ROWS, 8),
    )

    def inside(step):
        return jnp.logical_and(z + step >= 0, z + step < LEVELS)

    def send_halo(tall, which):
        for m, (step, here, there, rows) in enumerate(moves):

            @pl.when(inside(step))
            def _(m=m, step=step, here=here, there=there, rows=rows):
                remote(
                    tall.at[pl.ds(here, rows)],
                    tall.at[pl.ds(there, rows)],
                    halo_send.at[which, m],
                    halo_recv.at[which, m],
                    (z + step) * PLACES + place,
                    y,
                ).start()

    def wait_halo(tall, which):
        for m, (step, here, there, rows) in enumerate(moves):

            @pl.when(inside(-step))
            def _(m=m, there=there, rows=rows):
                wait_bytes(tall.at[pl.ds(there, rows)], halo_recv.at[which, m])

            @pl.when(jnp.logical_not(inside(-step)))
            def _(there=there, rows=rows):
                tall[pl.ds(there, rows)] = jnp.zeros((rows, GROUP, W), BF16)

    @pl.when(works)
    def _():
        v_half = taps[1, pl.ds(pl.multiple_of(place * GROUP, GROUP), GROUP), :]
        for t in range(K):
            v_taps[t] = jnp.broadcast_to(v_half[:, t : t + 1], (GROUP, W))
        wait_bytes(tall_s.at[pl.ds(HALO, 14)], rows_recv.at[0])
        wait_bytes(tall_s.at[pl.ds(HALO, 2)], here_sem.at[0])
        send_halo(tall_s, 0)
        wait_bytes(tall_f.at[pl.ds(HALO, 14)], rows_recv.at[1])
        wait_bytes(tall_f.at[pl.ds(HALO, 2)], here_sem.at[2])
        send_halo(tall_f, 1)

    load_in.wait()
    load_out.wait()

    @pl.when(points)
    def _():
        gain[...] = jnp.broadcast_to(gain_ref[...], (W, C)).T

        @loop(HID // BLOCK)
        def _(i):
            at = pl.ds(pl.multiple_of(i * BLOCK, BLOCK), BLOCK)
            w_in_t[at, :] = w_in[:, at].T
            w_out_t[:, at] = w_out[at, :].T

        wait_bytes(cell_grads.at[pl.ds(0, 3)], cot_recv)
        wait_bytes(cell_grads.at[0], here_sem.at[1])
        upstream = cell_grads[...].reshape(C, W)

        @loop(HID // BLOCK)
        def _(i):
            at = pl.ds(pl.multiple_of(i * BLOCK, BLOCK), BLOCK)
            grad_act[at, :] = jnp.dot(w_out[at, :], upstream, preferred_element_type=F32)

    def row_convolution(wide):
        def tap(t, acc):
            return acc + v_taps[t][None] * wide[pl.ds(t + 1, ROWS)]

        return lax.fori_loop(0, K, tap, jnp.zeros((ROWS, GROUP, W), F32))

    @pl.when(works)
    def _():
        wait_halo(tall_s, 0)
        wide_s[...] = tall_s[...].astype(F32)
        mixed[...] = row_convolution(wide_s).astype(BF16)

        @loop(ROWS)
        def _(r):
            go(
                jnp.logical_and(points, r == my_row),
                mixed.at[r],
                cell_values.at[y * GROUPS + place],
                mix_send,
                mix_recv,
                here_sem.at[3],
                level + r // 2,
                r % COUNT_Y,
            )

    @pl.when(points)
    def _():
        @pl.when(works)
        def _():
            wait_bytes(cell_values.at[pl.ds(0, C // GROUP - 1)], mix_recv)
            wait_bytes(cell_values.at[0], here_sem.at[3])

        @pl.when(idles)
        def _():
            wait_bytes(cell_values, mix_recv)

        values = cell_values[...].reshape(C, W).astype(F32)
        centred = values - jnp.sum(values, axis=0, keepdims=True) * (1.0 / C)
        variance = jnp.sum(centred * centred, axis=0, keepdims=True) * (1.0 / C)
        inverse = lax.rsqrt(variance + EPSILON)
        scaled = centred * inverse
        standard[...] = scaled
        inverse_rows[...] = inverse
        normed[...] = (scaled * gain[...]).astype(BF16)

        @loop(HID // BLOCK)
        def _(i):
            at = pl.ds(pl.multiple_of(i * BLOCK, BLOCK), BLOCK)
            pre = jnp.dot(w_in_t[at, :], normed[...], preferred_element_type=F32)
            cumulative = 0.5 * (1.0 + lax.erf(pre * ROOT_HALF))
            activated[at, :] = (pre * cumulative).astype(BF16)
            density = jnp.exp(-0.5 * pre * pre) * INV_ROOT_TWO_PI
            grad_pre[at, :] = (grad_act[at, :] * (cumulative + pre * density)).astype(BF16)

        scaled = jnp.dot(w_in[...], grad_pre[...], preferred_element_type=F32) * gain[...]
        mean_scaled = jnp.sum(scaled, axis=0, keepdims=True) * (1.0 / C)
        mean_product = jnp.sum(scaled * standard[...], axis=0, keepdims=True) * (1.0 / C)
        back = (scaled - mean_scaled - standard[...] * mean_product) * inverse_rows[...]
        grad_cells[...] = back.astype(BF16).reshape(C // GROUP, GROUP, W)

        @loop(C // GROUP)
        def _(i):
            to_y = i // GROUPS
            to_place = i % GROUPS
            go(
                jnp.logical_and(to_y == y, to_place == place),
                grad_cells.at[i],
                grad_rows.at[my_row],
                back_send,
                back_recv,
                here_sem.at[4],
                level + to_place,
                to_y,
            )

        branch = jnp.dot(w_out_t[...], activated[...], preferred_element_type=F32)
        branch_cells[...] = branch.astype(BF16).reshape(COUNT_Y, LOCAL, W)

        @loop(COUNT_Y)
        def _(i):
            go(
                i == y,
                branch_cells.at[i],
                branch_rows.at[y % 2],
                branch_send,
                branch_recv,
                here_sem.at[5],
                band,
                i,
            )

    lane = lax.broadcasted_iota(jnp.int32, (GROUP, W), 1)

    @pl.when(works)
    def _():
        wait_halo(tall_f, 1)
        wide_f[...] = tall_f[...].astype(F32)
        rows_f = row_convolution(wide_f)
        column = lax.broadcasted_iota(jnp.int32, (ROWS * GROUP, W), 1)
        rows_f = rows_f.reshape(ROWS * GROUP, W)

        @loop(K)
        def _(t):
            moved = pltpu.roll(rows_f, lax.rem(W + RADIUS - t, W), 1)
            first = column + (t - RADIUS)
            moved = jnp.where(jnp.logical_and(first >= 0, first < W), moved, 0.0)
            shifted[t] = moved.reshape(ROWS, GROUP, W)

        @pl.when(points)
        def _():
            wait_bytes(grad_rows.at[pl.ds(0, ROWS - 1)], back_recv)
            wait_bytes(grad_rows.at[0], here_sem.at[4])

        @pl.when(rests)
        def _():
            wait_bytes(grad_rows, back_recv)

        grads = grad_rows[...].astype(F32)

        def tap(t, sums):
            v_sum = jnp.sum(grads * wide_s[pl.ds(t + 1, ROWS)], axis=0)
            h_sum = jnp.sum(grads * shifted[t], axis=0)
            sums = jnp.where(lane == t, jnp.sum(v_sum, axis=1, keepdims=True), sums)
            return jnp.where(lane == t + 64, jnp.sum(h_sum, axis=1, keepdims=True), sums)

        sums = lax.fori_loop(0, K, tap, jnp.zeros((GROUP, W), F32))
        partial[...] = sums
        partials[z] = sums

        @loop(LEVELS)
        def _(i):
            @pl.when(i != z)
            def _():
                remote(
                    partial,
                    partials.at[z],
                    sum_send,
                    sum_recv,
                    i * PLACES + place,
                    y,
                ).start()

    @pl.when(points)
    def _():
        wait_bytes(branch_rows.at[0], branch_recv)
        wait_bytes(branch_rows.at[0], here_sem.at[5])

    @pl.when(rests)
    def _():
        wait_bytes(branch_rows, branch_recv)

    for row in range(2):
        added = f_ref[:, row].reshape(LOCAL, W).astype(F32) + branch_rows[row].astype(F32)
        out_ref[row] = added.astype(BF16)

    @pl.when(works)
    def _():
        wait_bytes(partials.at[pl.ds(0, LEVELS - 1)], sum_recv)
        grads = partials[0]
        for i in range(1, LEVELS):
            grads = grads + partials[i]
        squares = jnp.sum(grads * grads, axis=1, keepdims=True) / (2 * K)
        steps = STEP_SIZE * grads * lax.rsqrt(squares + EPSILON)
        update[...] = steps
        updates[place] = steps

        @loop(PLACES)
        def _(i):
            @pl.when(i != place)
            def _():
                remote(
                    update,
                    updates.at[place],
                    all_send,
                    all_recv,
                    level + i,
                    y,
                ).start()

        wait_bytes(updates.at[pl.ds(0, GROUPS - 1)], all_recv)

    @pl.when(idles)
    def _():
        wait_bytes(updates.at[pl.ds(0, GROUPS)], all_recv)

    up_ref[...] = updates[...].reshape(W, W).T

    @pl.when(works)
    def _():
        for which, tall in enumerate((tall_s, tall_f)):
            wait_bytes(tall.at[pl.ds(0, 10)], rows_send.at[which])
            for m, (step, here, there, rows) in enumerate(moves):

                @pl.when(inside(step))
                def _(m=m, tall=tall, which=which, here=here, rows=rows):
                    wait_bytes(tall.at[pl.ds(here, rows)], halo_send.at[which, m])

        @pl.when(points)
        def _():
            wait_bytes(mixed.at[pl.ds(0, ROWS - 1)], mix_send)
            wait_bytes(grad_cells.at[pl.ds(0, C // GROUP - 1)], back_send)

        @pl.when(rests)
        def _():
            wait_bytes(mixed, mix_send)

        wait_bytes(partials.at[pl.ds(0, LEVELS - 1)], sum_send)
        wait_bytes(updates.at[pl.ds(0, PLACES - 1)], all_send)

    @pl.when(idles)
    def _():
        for which, tall in enumerate((tall_s, tall_f)):
            wait_bytes(tall.at[pl.ds(0, 12)], rows_send.at[which])

        @pl.when(points)
        def _():
            wait_bytes(grad_cells, back_send)

    @pl.when(points)
    def _():
        wait_bytes(cell_grads.at[0], cot_send)
        wait_bytes(branch_cells.at[pl.ds(0, COUNT_Y - 1)], branch_send)

    @pl.when(rests)
    def _():
        wait_bytes(cell_grads.at[pl.ds(0, 2)], cot_send)


def local(
    features,
    h_kernel,
    v_kernel,
    h_kernel_avg,
    v_kernel_avg,
    norm_gain,
    w_in,
    w_out,
    cotangent,
    tissue,
):
    grouped = jnp.transpose(features.reshape(GROUPS, GROUP, 2, W), (0, 2, 1, 3))
    weighted = jnp.transpose(cotangent * tissue.astype(BF16)[None], (1, 0, 2))
    vmem = pl.BlockSpec(memory_space=pltpu.VMEM)
    hbm = pl.BlockSpec(memory_space=pl.ANY)
    dma = pltpu.SemaphoreType.DMA
    out, step = pl.pallas_call(
        kernel,
        name="swa_step",
        out_shape=(
            jax.ShapeDtypeStruct((2, LOCAL, W), BF16),
            jax.ShapeDtypeStruct((W, W), F32),
        ),
        in_specs=[vmem] * 5 + [hbm] * 2,
        out_specs=(vmem, vmem),
        scratch_shapes=[
            pltpu.VMEM((C, HID), BF16),
            pltpu.VMEM((HID, C), BF16),
            pltpu.VMEM((HID, C), BF16),
            pltpu.VMEM((C, HID), BF16),
            pltpu.VMEM((C, W), F32),
            pltpu.VMEM((2, W, W), F32),
            pltpu.VMEM((GROUPS, 2, GROUP, W), BF16),
            pltpu.VMEM((TALL, GROUP, W), BF16),
            pltpu.VMEM((TALL, GROUP, W), BF16),
            pltpu.VMEM((TALL, GROUP, W), F32),
            pltpu.VMEM((TALL, GROUP, W), F32),
            pltpu.VMEM((K, GROUP, W), F32),
            pltpu.VMEM((K, ROWS, GROUP, W), F32),
            pltpu.VMEM((ROWS, GROUP, W), BF16),
            pltpu.VMEM((COUNT_Y, LOCAL, W), BF16),
            pltpu.VMEM((HID, W), F32),
            pltpu.VMEM((C // GROUP, GROUP, W), BF16),
            pltpu.VMEM((C, W), F32),
            pltpu.VMEM((1, W), F32),
            pltpu.VMEM((C, W), BF16),
            pltpu.VMEM((HID, W), BF16),
            pltpu.VMEM((HID, W), BF16),
            pltpu.VMEM((C // GROUP, GROUP, W), BF16),
            pltpu.VMEM((ROWS, GROUP, W), BF16),
            pltpu.VMEM((COUNT_Y, LOCAL, W), BF16),
            pltpu.VMEM((2, LOCAL, W), BF16),
            pltpu.VMEM((GROUP, W), F32),
            pltpu.VMEM((LEVELS, GROUP, W), F32),
            pltpu.VMEM((GROUP, W), F32),
            pltpu.VMEM((PLACES, GROUP, W), F32),
            dma((2,)),
            dma((6,)),
            dma((2,)),
            dma((2,)),
            dma((2, 4)),
            dma((2, 4)),
            dma,
            dma,
            dma,
            dma,
            dma,
            dma,
            dma,
            dma,
            dma,
            dma,
            dma,
            dma,
        ],
        compiler_params=pltpu.CompilerParams(collective_id=0, has_side_effects=True),
    )(
        grouped,
        weighted,
        h_kernel.T,
        v_kernel.T,
        norm_gain.reshape(1, C),
        w_in,
        w_out,
    )
    block_out = jnp.transpose(out, (1, 0, 2))
    v_new = v_kernel - step[0:K, 0:LOCAL].T
    h_new = h_kernel - step[64 : 64 + K, 0:LOCAL].T
    h_swa = (AVERAGED * h_kernel_avg + h_new) / (AVERAGED + 1)
    v_swa = (AVERAGED * v_kernel_avg + v_new) / (AVERAGED + 1)
    return (block_out, h_new, v_new, h_swa, v_swa)


def solution(mesh):
    return jax.shard_map(
        local,
        mesh=mesh,
        in_specs=(
            P("chan", "band", None),
            P("chan", None),
            P("chan", None),
            P("chan", None),
            P("chan", None),
            P(),
            P(),
            P(),
            P("chan", "band", None),
            P("band", None),
        ),
        out_specs=(
            P("chan", "band", None),
            P("chan", None),
            P("chan", None),
            P("chan", None),
            P("chan", None),
        ),
        check_vma=False,
    )
```

time: 640 us -> 69.7 us (0.11)
  blocking collectives: 487 us -> 0 us
  waiting for transfers between devices: 72.9 us -> 0 us
  Pallas kernels: 0 us -> 60.9 us
  starting transfers between devices: 56.2 us -> 0 us
  matrix products: 8.12 us -> 0 us
    psum x1 -> x0, blocking collectives: 487 us -> none  [local(): h_grad, v_grad = lax.psum((h_grad, v_grad), 'band')]
    all_to_all x8 -> x0, waiting for transfers between devices: 72.9 us -> none  [the longest x1 14.7 us: local(): lax.all_to_all(split_rows(smoothed), 'band', split_axis=2, concat_axis=1,...]
    pallas_call x0 -> x1, Pallas kernels: none -> 60.9 us  [local(): pl.pallas_call(kernel, name='swa_step', out_shape=(jax.ShapeDtypeStruct((...]
    all_to_all x8 -> x0, starting transfers between devices: 56.2 us -> none  [the longest x1 20.4 us: local(): lax.all_to_all(split_rows(smoothed), 'band', split_axis=2, concat_axis=1,...]
    conv_general_dilated x5 -> x0, matrix products: 6.49 us -> none  [the longest x3 5.12 us: along_last(): lax.conv_general_dilated(source[None], kernel[:, None, None, :], (1, 1),...]
  transfers between devices with their start and end apart: 8 -> 0, of which waited for: 8 -> 0; matrix products, arithmetic and copies ran while one was open for 1% -> 0% of each run, Pallas kernels for 0% -> 0%
where the time goes in v1:
time: 69.7 us; the launch traced here: 69.2 us
  Pallas kernels  60.9 us (87%)
  local copies, waits for them, and re-layouts  4.14 us (6%)
  other arithmetic  3.51 us (5%)
    pallas_call x1, Pallas kernels, local(): pl.pallas_call(kernel, name='swa_step', out_shape=(jax.ShapeDtypeStruct((...  60.9 us
    unnamed x9, local copies, waits for them, and re-layouts  1.47 us
    reshape x1, local copies, waits for them, and re-layouts, local(): grouped = jnp.transpose(features.reshape(GROUPS, GROUP, 2, W), (0, 2, 1, 3))  1.42 us
    transpose x1, other arithmetic, local(): weighted = jnp.transpose(cotangent * tissue.astype(BF16)[None], (1, 0, 2))  1.42 us
    div x1, other arithmetic, local(): v_swa = (AVERAGED * v_kernel_avg + v_new) / (AVERAGED + 1)  1.4 us

profile of v1, /device:TPU:1, one launch (start us, length us, event | category | flops | bytes accessed | tf_op | source)
XLA Modules:
  0.0 69.2 jit_solution(3219855037848369110)
XLA Ops:
  0.6 0.7 convert_element_type.3
  1.3 1.2 %reshape.18.gain_ref = f32[1,384]{1,0:T(1,128)} reshape(f32[384]{0:T(512)} %param.15) | data formatting | bytes 3072 | tf_op jit(solution)/shard_map/reshape | solution.py:609
  2.6 1.4 %fusion.w_ref = bf16[2,96,128]{2,1,0:T(8,128)(2,1)} fusion(bf16[96,2,128]{2,1,0:T(2,128)(2,1)} %param.18, bf16[2,128]{1,0:T(2,128)(2,1)S(1)} %convert_element_type.3), kind=kLoop, calls=%fused_computation.2 | loop fusion | flops 24576 | bytes 98816 | tf_op jit(solution)/shard_map/transpose | solution.py:540
  4.0 1.4 %copy.27 = bf16[6,16,2,128]{3,1,2,0:T(8,128)(2,1)} copy(bf16[6,16,2,128]{3,2,1,0:T(2,128)(2,1)} %bitcast.18) | data formatting | bytes 98304 | tf_op jit(solution)/shard_map/reshape | solution.py:539
  5.4 0.0 copy-start
  5.4 0.0 copy-start.1
  5.4 0.0 copy-start.2
  5.4 0.0 copy-start.3
  5.4 60.9 %swa_step.1 = (bf16[2,96,128]{2,1,0:T(8,128)(2,1)}, f32[128,128]{1,0:T(8,128)}) custom-call(bf16[6,2,16,128]{3,2,1,0:T(8,128)(2,1)} %bitcast.15, bf16[2,96,128]{2,1,0:T(8,128)(2,1)} %fusion.w_ref, f32[47,96]{1,0:T(8,128)} %bitcast.16, f32[47,96]{1,0:T(8,128)} %bitcast.17, f32[1,384]{1,0:T(1,128)} %reshape.18.gain_ref, bf16[384,1536]{1,0:T(8,128)(2,1)} %w_in_hbm.1, ...), custom_call_target="tpu_custom_call" | custom-call | tf_op jit(solution)/shard_map/swa_step/pallas_call | solution.py:544
  66.4 1.5 %copy.20 = bf16[96,2,128]{2,1,0:T(2,128)(2,1)} copy(bf16[96,2,128]{2,0,1:T(8,128)(2,1)} %bitcast.19) | data formatting | bytes 98304
  67.8 0.0 copy-done
  67.8 0.0 copy-done.1
  67.8 0.0 copy-done.2
  67.8 0.0 copy-done.3
  67.8 1.4 %add_multiply_fusion = (f32[96,47]{0,1:T(8,128)}, f32[96,47]{0,1:T(8,128)}, f32[96,47]{0,1:T(8,128)}, f32[96,47]{0,1:T(8,128)}) fusion(f32[96,47]{0,1:T(8,128)S(1)} %copy-done.2, f32[96,47]{0,1:T(8,128)S(1)} %copy-done.1, f32[128,128]{1,0:T(8,128)} %get-tuple-element.8, f32[96,47]{0,1:T(8,128)S(1)} %copy-done, f32[96,47]{0,1:T(8,128)S(1)} %copy-done.3), kind=kLoop, calls=%fused_computation.5 | loop fusion | flops 36096 | bytes 180480 | tf_op jit(solution)/shard_map/div | solution.py:617
Async XLA Ops:
  5.4 62.4 %copy-start = (f32[96,47]{0,1:T(8,128)S(1)}, f32[96,47]{0,1:T(8,128)}, u32[]{:S(2)}) copy-start(f32[96,47]{0,1:T(8,128)} %param.11) | copy-start | bytes 54148
  5.4 62.4 %copy-start.1 = (f32[96,47]{0,1:T(8,128)S(1)}, f32[96,47]{0,1:T(8,128)}, u32[]{:S(2)}) copy-start(f32[96,47]{0,1:T(8,128)} %param.12) | copy-start | bytes 54148
  5.4 62.4 %copy-start.2 = (f32[96,47]{0,1:T(8,128)S(1)}, f32[96,47]{0,1:T(8,128)}, u32[]{:S(2)}) copy-start(f32[96,47]{0,1:T(8,128)} %param.14) | copy-start | bytes 54148
  5.4 62.4 %copy-start.3 = (f32[96,47]{0,1:T(8,128)S(1)}, f32[96,47]{0,1:T(8,128)}, u32[]{:S(2)}) copy-start(f32[96,47]{0,1:T(8,128)} %param.13) | copy-start | bytes 54148

commit v2 on v1

--- a/solution.py
+++ b/solution.py
@@ -39,8 +39,9 @@
 
 
 def kernel(
-    f_ref,
-    w_ref,
+    f_hbm,
+    cot_hbm,
+    tissue_ref,
     h_ref,
     v_ref,
     gain_ref,
@@ -48,6 +49,10 @@
     w_out_hbm,
     out_ref,
     up_ref,
+    f_pairs,
+    cot_pairs,
+    f_rows,
+    w_rows,
     w_in,
     w_out,
     w_in_t,
@@ -78,6 +83,7 @@
     partials,
     update,
     updates,
+    far_sem,
     load_sem,
     here_sem,
     rows_send,
@@ -144,18 +150,23 @@
                 barrier, 1, device_id=(level + to_place, to_y), device_id_type=MESH
             )
 
-    @loop(LEVELS)
-    def _(i):
-        @pl.when(jnp.logical_and(works, i != z))
-        def _():
-            pl.semaphore_signal(
-                barrier, 1, device_id=(i * PLACES + place, y), device_id_type=MESH
-            )
+    def tell(sem, step):
+        there = lax.rem(z + step + LEVELS, LEVELS)
+        pl.semaphore_signal(
+            sem, 1, device_id=(there * PLACES + place, y), device_id_type=MESH
+        )
+
+    @pl.when(works)
+    def _():
+        for step in (1, -1, 2, -2):
+            tell(barrier, step)
 
     load_in = pltpu.make_async_copy(w_in_hbm, w_in, load_sem.at[0])
     load_out = pltpu.make_async_copy(w_out_hbm, w_out, load_sem.at[1])
-    load_in.start()
-    load_out.start()
+    load_f = pltpu.make_async_copy(f_hbm, f_pairs, load_sem.at[2])
+    load_cot = pltpu.make_async_copy(cot_hbm, cot_pairs, load_sem.at[3])
+    for load in (load_f, load_cot, load_in, load_out):
+        load.start()
 
     taps[...] = jnp.zeros((2, W, W), F32)
     taps[0, 0:K, 0:LOCAL] = h_ref[...]
@@ -163,7 +174,10 @@
     h_half = taps[0].T[0:LOCAL].astype(BF16).astype(F32)
     taps[1] = taps[1].T.astype(BF16).astype(F32)
     column = lax.broadcasted_iota(jnp.int32, (LOCAL, W), 1)
-    sources = [f_ref[:, row].reshape(LOCAL, W).astype(F32) for row in range(2)]
+    load_f.wait()
+    sources = [f_pairs[:, row, :].astype(F32) for row in range(2)]
+    for row in range(2):
+        f_rows[:, row] = sources[row].astype(BF16).reshape(GROUPS, GROUP, W)
     sums = [jnp.zeros((LOCAL, W), F32) for row in range(2)]
     for t in range(K):
         weight = jnp.broadcast_to(h_half[:, t : t + 1], (LOCAL, W))
@@ -178,10 +192,16 @@
             sums[row] = sums[row] + weight * moved
     for row in range(2):
         smoothed[:, row] = sums[row].astype(BF16).reshape(GROUPS, GROUP, W)
+    load_cot.wait()
+    for row in range(2):
+        mask = tissue_ref[row : row + 1, :].astype(F32)
+        w_rows[row] = (cot_pairs[:, row, :].astype(F32) * mask).astype(BF16)
 
     @pl.when(works)
     def _():
-        pl.semaphore_wait(barrier, PLACES * COUNT_Y - 1 + LEVELS - 1)
+        pl.semaphore_wait(barrier, PLACES * COUNT_Y - 1 + 4)
+        tell(far_sem.at[0], 2)
+        tell(far_sem.at[0], -2)
 
     @pl.when(idles)
     def _():
@@ -205,7 +225,7 @@
     for row in range(2):
         go(
             jnp.logical_and(points, y % 2 == row),
-            w_ref.at[row],
+            w_rows.at[row],
             cell_grads.at[y],
             cot_send,
             cot_recv,
@@ -218,7 +238,7 @@
     def _(g):
         go(
             g == place,
-            f_ref.at[g],
+            f_rows.at[g],
             tall_f.at[own_pair],
             rows_send.at[1],
             rows_recv.at[1],
@@ -279,7 +299,8 @@
 
     @pl.when(points)
     def _():
-        gain[...] = jnp.broadcast_to(gain_ref[...], (W, C)).T
+        for i in range(C // W):
+            gain[i * W : (i + 1) * W] = jnp.broadcast_to(gain_ref[i : i + 1, :], (W, W)).T
 
         @loop(HID // BLOCK)
         def _(i):
@@ -296,11 +317,15 @@
             at = pl.ds(pl.multiple_of(i * BLOCK, BLOCK), BLOCK)
             grad_act[at, :] = jnp.dot(w_out[at, :], upstream, preferred_element_type=F32)
 
+
     def row_convolution(wide):
         def tap(t, acc):
             return acc + v_taps[t][None] * wide[pl.ds(t + 1, ROWS)]
 
-        return lax.fori_loop(0, K, tap, jnp.zeros((ROWS, GROUP, W), F32))
+        acc = jnp.zeros((ROWS, GROUP, W), F32)
+        for t in range(K):
+            acc = tap(t, acc)
+        return acc
 
     @pl.when(works)
     def _():
@@ -320,6 +345,7 @@
                 level + r // 2,
                 r % COUNT_Y,
             )
+
 
     @pl.when(points)
     def _():
@@ -387,10 +413,14 @@
                 i,
             )
 
+
     lane = lax.broadcasted_iota(jnp.int32, (GROUP, W), 1)
 
     @pl.when(works)
     def _():
+        pl.semaphore_wait(far_sem.at[0], 2)
+        tell(far_sem.at[1], 4)
+        tell(far_sem.at[1], -4)
         wait_halo(tall_f, 1)
         wide_f[...] = tall_f[...].astype(F32)
         rows_f = row_convolution(wide_f)
@@ -421,9 +451,12 @@
             sums = jnp.where(lane == t, jnp.sum(v_sum, axis=1, keepdims=True), sums)
             return jnp.where(lane == t + 64, jnp.sum(h_sum, axis=1, keepdims=True), sums)
 
-        sums = lax.fori_loop(0, K, tap, jnp.zeros((GROUP, W), F32))
-        partial[...] = sums
-        partials[z] = sums
+        sums = jnp.zeros((GROUP, W), F32)
+        for t in range(K):
+            sums = tap(t, sums)
+        partial[...] = sums.astype(BF16)
+        partials[z] = sums.astype(BF16)
+        pl.semaphore_wait(far_sem.at[1], 2)
 
         @loop(LEVELS)
         def _(i):
@@ -438,6 +471,7 @@
                     y,
                 ).start()
 
+
     @pl.when(points)
     def _():
         wait_bytes(branch_rows.at[0], branch_recv)
@@ -448,15 +482,13 @@
         wait_bytes(branch_rows, branch_recv)
 
     for row in range(2):
-        added = f_ref[:, row].reshape(LOCAL, W).astype(F32) + branch_rows[row].astype(F32)
+        added = f_rows[:, row].reshape(LOCAL, W).astype(F32) + branch_rows[row].astype(F32)
         out_ref[row] = added.astype(BF16)
 
     @pl.when(works)
     def _():
         wait_bytes(partials.at[pl.ds(0, LEVELS - 1)], sum_recv)
-        grads = partials[0]
-        for i in range(1, LEVELS):
-            grads = grads + partials[i]
+        grads = jnp.sum(partials[...].astype(F32), axis=0)
         squares = jnp.sum(grads * grads, axis=1, keepdims=True) / (2 * K)
         steps = STEP_SIZE * grads * lax.rsqrt(squares + EPSILON)
         update[...] = steps
@@ -524,6 +556,19 @@
         wait_bytes(cell_grads.at[pl.ds(0, 2)], cot_send)
 
 
+def finish(
+    out_rows, step_ref, h_ref, v_ref, h_avg, v_avg, out_ref, h_new, v_new, h_swa, v_swa
+):
+    for row in range(2):
+        out_ref[:, row, :] = out_rows[row]
+    new = h_ref[...] - step_ref[64 : 64 + K, 0:LOCAL]
+    h_new[...] = new
+    h_swa[...] = (AVERAGED * h_avg[...] + new) / (AVERAGED + 1)
+    new = v_ref[...] - step_ref[0:K, 0:LOCAL]
+    v_new[...] = new
+    v_swa[...] = (AVERAGED * v_avg[...] + new) / (AVERAGED + 1)
+
+
 def local(
     features,
     h_kernel,
@@ -536,8 +581,6 @@
     cotangent,
     tissue,
 ):
-    grouped = jnp.transpose(features.reshape(GROUPS, GROUP, 2, W), (0, 2, 1, 3))
-    weighted = jnp.transpose(cotangent * tissue.astype(BF16)[None], (1, 0, 2))
     vmem = pl.BlockSpec(memory_space=pltpu.VMEM)
     hbm = pl.BlockSpec(memory_space=pl.ANY)
     dma = pltpu.SemaphoreType.DMA
@@ -548,9 +591,13 @@
             jax.ShapeDtypeStruct((2, LOCAL, W), BF16),
             jax.ShapeDtypeStruct((W, W), F32),
         ),
-        in_specs=[vmem] * 5 + [hbm] * 2,
+        in_specs=[hbm] * 2 + [vmem] * 4 + [hbm] * 2,
         out_specs=(vmem, vmem),
         scratch_shapes=[
+            pltpu.VMEM((LOCAL, 2, W), BF16),
+            pltpu.VMEM((LOCAL, 2, W), BF16),
+            pltpu.VMEM((GROUPS, 2, GROUP, W), BF16),
+            pltpu.VMEM((2, LOCAL, W), BF16),
             pltpu.VMEM((C, HID), BF16),
             pltpu.VMEM((HID, C), BF16),
             pltpu.VMEM((HID, C), BF16),
@@ -577,11 +624,12 @@
             pltpu.VMEM((ROWS, GROUP, W), BF16),
             pltpu.VMEM((COUNT_Y, LOCAL, W), BF16),
             pltpu.VMEM((2, LOCAL, W), BF16),
-            pltpu.VMEM((GROUP, W), F32),
-            pltpu.VMEM((LEVELS, GROUP, W), F32),
+            pltpu.VMEM((GROUP, W), BF16),
+            pltpu.VMEM((LEVELS, GROUP, W), BF16),
             pltpu.VMEM((GROUP, W), F32),
             pltpu.VMEM((PLACES, GROUP, W), F32),
-            dma((2,)),
+            pltpu.SemaphoreType.REGULAR((2,)),
+            dma((4,)),
             dma((6,)),
             dma((2,)),
             dma((2,)),
@@ -602,20 +650,24 @@
         ],
         compiler_params=pltpu.CompilerParams(collective_id=0, has_side_effects=True),
     )(
-        grouped,
-        weighted,
+        features,
+        cotangent,
+        tissue,
         h_kernel.T,
         v_kernel.T,
-        norm_gain.reshape(1, C),
+        norm_gain.reshape(C // W, W),
         w_in,
         w_out,
     )
-    block_out = jnp.transpose(out, (1, 0, 2))
-    v_new = v_kernel - step[0:K, 0:LOCAL].T
-    h_new = h_kernel - step[64 : 64 + K, 0:LOCAL].T
-    h_swa = (AVERAGED * h_kernel_avg + h_new) / (AVERAGED + 1)
-    v_swa = (AVERAGED * v_kernel_avg + v_new) / (AVERAGED + 1)
-    return (block_out, h_new, v_new, h_swa, v_swa)
+    taps = jax.ShapeDtypeStruct((K, LOCAL), F32)
+    block_out, h_new, v_new, h_swa, v_swa = pl.pallas_call(
+        finish,
+        name="finish",
+        out_shape=(jax.ShapeDtypeStruct((LOCAL, 2, W), BF16), taps, taps, taps, taps),
+        in_specs=[vmem] * 6,
+        out_specs=(vmem,) * 5,
+    )(out, step, h_kernel.T, v_kernel.T, h_kernel_avg.T, v_kernel_avg.T)
+    return (block_out, h_new.T, v_new.T, h_swa.T, v_swa.T)
 
 
 def solution(mesh):

time: 69.7 us -> 55.8 us (0.80)
  Pallas kernels: 60.9 us -> 54.9 us
  local copies, waits for them, and re-layouts: 4.14 us -> 0 us
  other arithmetic: 3.51 us -> 0 us
    pallas_call x1, Pallas kernels: 60.9 us -> 53.3 us  [local(): pl.pallas_call(kernel, name='swa_step', out_shape=(jax.ShapeDtypeStruct((...]
    reshape x2 -> x0, local copies, waits for them, and re-layouts: 2.67 us -> none  [the longest x1 1.42 us: local(): grouped = jnp.transpose(features.reshape(GROUPS, GROUP, 2, W), (0, 2, 1, 3))]
    pallas_call x0 -> x1, Pallas kernels: none -> 1.64 us  [local(): pl.pallas_call(finish, name='finish', out_shape=(jax.ShapeDtypeStruct((LO...]
    unnamed x9 -> x0, local copies, waits for them, and re-layouts: 1.47 us -> none
    transpose x1 -> x0, other arithmetic: 1.42 us -> none  [local(): weighted = jnp.transpose(cotangent * tissue.astype(BF16)[None], (1, 0, 2))]
    div x1 -> x0, other arithmetic: 1.4 us -> none  [local(): v_swa = (AVERAGED * v_kernel_avg + v_new) / (AVERAGED + 1)]
where the time goes in v2:
time: 55.8 us; the launch traced here: 55.6 us
  Pallas kernels  54.9 us (98%)
  between operations  0.64 us (1%)
    pallas_call x1, Pallas kernels, local(): pl.pallas_call(kernel, name='swa_step', out_shape=(jax.ShapeDtypeStruct((...  53.3 us
    pallas_call x1, Pallas kernels, local(): pl.pallas_call(finish, name='finish', out_shape=(jax.ShapeDtypeStruct((LO...  1.64 us

profile of v2, /device:TPU:1, one launch (start us, length us, event | category | flops | bytes accessed | tf_op | source)
XLA Modules:
  0.0 55.6 jit_solution(5084363221155756735)
XLA Ops:
  0.6 53.3 %swa_step.1 = (bf16[2,96,128]{2,1,0:T(8,128)(2,1)}, f32[128,128]{1,0:T(8,128)}) custom-call(bf16[96,2,128]{2,1,0:T(2,128)(2,1)} %f_hbm.1, bf16[96,2,128]{2,1,0:T(2,128)(2,1)} %cot_hbm.1, s32[2,128]{1,0:T(2,128)} %tissue_ref.1, f32[47,96]{1,0:T(8,128)} %bitcast.9, f32[47,96]{1,0:T(8,128)} %bitcast.11, f32[3,128]{1,0:T(4,128)} %bitcast.15, ...), custom_call_target="tpu_custom_call" | custom-call | tf_op jit(solution)/shard_map/swa_step/pallas_call | solution.py:587
  53.9 1.6 %finish.1 = (bf16[96,2,128]{2,1,0:T(2,128)(2,1)}, f32[47,96]{1,0:T(8,128)}, f32[47,96]{1,0:T(8,128)}, f32[47,96]{1,0:T(8,128)}, f32[47,96]{1,0:T(8,128)}) custom-call(bf16[2,96,128]{2,1,0:T(8,128)(2,1)} %get-tuple-element.12.out_rows, f32[128,128]{1,0:T(8,128)} %get-tuple-element.13.step_ref, f32[47,96]{1,0:T(8,128)} %bitcast.10, f32[47,96]{1,0:T(8,128)} %bitcast.12, ...), custom_call_target="tpu_custom_call" | custom-call | tf_op jit(solution)/shard_map/finish/pallas_call | solution.py:663

commit v3 on v2

--- a/solution.py
+++ b/solution.py
@@ -41,14 +41,19 @@
 def kernel(
     f_hbm,
     cot_hbm,
+    tissue_hbm,
+    h_hbm,
+    v_hbm,
+    gain_hbm,
+    w_in_hbm,
+    w_out_hbm,
+    out_hbm,
+    updates,
     tissue_ref,
     h_ref,
     v_ref,
     gain_ref,
-    w_in_hbm,
-    w_out_hbm,
-    out_ref,
-    up_ref,
+    out_rows,
     f_pairs,
     cot_pairs,
     f_rows,
@@ -82,7 +87,6 @@
     partial,
     partials,
     update,
-    updates,
     far_sem,
     load_sem,
     here_sem,
@@ -135,20 +139,16 @@
             remote(src, dst, send, recv, to_band, to_y).start()
 
     def loop(count):
-        return lambda body: lax.fori_loop(0, count, lambda i, c: (body(i), c)[1], 0)
+        return lambda body: [body(i) for i in range(count)]
 
     barrier = pltpu.get_barrier_semaphore()
 
-    @loop(PLACES * COUNT_Y)
-    def _(i):
-        to_place = i // COUNT_Y
-        to_y = i % COUNT_Y
-
-        @pl.when(jnp.logical_or(to_place != place, to_y != y))
-        def _():
-            pl.semaphore_signal(
-                barrier, 1, device_id=(level + to_place, to_y), device_id_type=MESH
-            )
+    for step in range(1, PLACES):
+        line = level + lax.rem(place + step, PLACES)
+        pl.semaphore_signal(barrier, 1, device_id=(line, y), device_id_type=MESH)
+    others = [lax.rem(y + step, COUNT_Y) for step in range(1, COUNT_Y)]
+    for to_y in others:
+        pl.semaphore_signal(barrier, 1, device_id=(band, to_y), device_id_type=MESH)
 
     def tell(sem, step):
         there = lax.rem(z + step + LEVELS, LEVELS)
@@ -165,9 +165,17 @@
     load_out = pltpu.make_async_copy(w_out_hbm, w_out, load_sem.at[1])
     load_f = pltpu.make_async_copy(f_hbm, f_pairs, load_sem.at[2])
     load_cot = pltpu.make_async_copy(cot_hbm, cot_pairs, load_sem.at[3])
-    for load in (load_f, load_cot, load_in, load_out):
+    small = [
+        pltpu.make_async_copy(src, dst, load_sem.at[4 + i])
+        for i, (src, dst) in enumerate(
+            ((h_hbm, h_ref), (v_hbm, v_ref), (tissue_hbm, tissue_ref), (gain_hbm, gain_ref))
+        )
+    ]
+    for load in (load_f, *small, load_cot, load_in, load_out):
         load.start()
 
+    for load in small:
+        load.wait()
     taps[...] = jnp.zeros((2, W, W), F32)
     taps[0, 0:K, 0:LOCAL] = h_ref[...]
     taps[1, 0:K, 0:LOCAL] = v_ref[...]
@@ -199,13 +207,16 @@
 
     @pl.when(works)
     def _():
-        pl.semaphore_wait(barrier, PLACES * COUNT_Y - 1 + 4)
+        pl.semaphore_wait(barrier, PLACES - 1 + COUNT_Y - 1 + 4)
         tell(far_sem.at[0], 2)
         tell(far_sem.at[0], -2)
 
     @pl.when(idles)
     def _():
-        pl.semaphore_wait(barrier, PLACES * COUNT_Y - 1)
+        pl.semaphore_wait(barrier, PLACES - 1 + COUNT_Y - 1)
+
+    for to_y in others:
+        pl.semaphore_signal(far_sem.at[2], 1, device_id=(band, to_y), device_id_type=MESH)
 
     own_pair = pl.ds(HALO + 2 * place, 2)
 
@@ -216,7 +227,7 @@
             smoothed.at[g],
             tall_s.at[own_pair],
             rows_send.at[0],
-            rows_recv.at[0],
+            rows_recv.at[place],
             here_sem.at[0],
             level + g,
             y,
@@ -241,7 +252,7 @@
             f_rows.at[g],
             tall_f.at[own_pair],
             rows_send.at[1],
-            rows_recv.at[1],
+            rows_recv.at[PLACES],
             here_sem.at[2],
             level + g,
             y,
@@ -287,15 +298,40 @@
         v_half = taps[1, pl.ds(pl.multiple_of(place * GROUP, GROUP), GROUP), :]
         for t in range(K):
             v_taps[t] = jnp.broadcast_to(v_half[:, t : t + 1], (GROUP, W))
-        wait_bytes(tall_s.at[pl.ds(HALO, 14)], rows_recv.at[0])
-        wait_bytes(tall_s.at[pl.ds(HALO, 2)], here_sem.at[0])
-        send_halo(tall_s, 0)
-        wait_bytes(tall_f.at[pl.ds(HALO, 14)], rows_recv.at[1])
-        wait_bytes(tall_f.at[pl.ds(HALO, 2)], here_sem.at[2])
-        send_halo(tall_f, 1)
+        for hop, flip in ((0, 0), (0, 1), (1, 0), (1, 1), (3, 0), (3, 1), (2, 0), (2, 1)):
+            source = lax.rem(place + 2 * hop, PLACES)
+            if flip:
+                source = source + 1 - 2 * core
+            pair = tall_s.at[pl.ds(HALO + 2 * source, 2)]
+            if hop == 0 and flip == 0:
+                wait_bytes(pair, here_sem.at[0])
+            else:
+                wait_bytes(pair, rows_recv.at[source])
+            upper = source >= PLACES // 2
+            far = jnp.where(upper, 2, -2)
+            far_row = jnp.where(upper, 2 * source - 8, HALO + 2 * ROWS + 2 * source)
+            far_m = jnp.where(upper, 2, 3)
+            for m, step, row in (
+                (far_m, far, far_row),
+                (0, 1, 8 + 2 * source),
+                (1, -1, HALO + ROWS + 2 * source),
+            ):
+
+                @pl.when(inside(step))
+                def _(m=m, step=step, row=row, pair=pair):
+                    remote(
+                        pair,
+                        tall_s.at[pl.ds(row, 2)],
+                        halo_send.at[0, m],
+                        halo_recv.at[0, m],
+                        (z + step) * PLACES + place,
+                        y,
+                    ).start()
+
 
     load_in.wait()
     load_out.wait()
+    pl.semaphore_wait(far_sem.at[2], COUNT_Y - 1)
 
     @pl.when(points)
     def _():
@@ -346,6 +382,9 @@
                 r % COUNT_Y,
             )
 
+        wait_bytes(tall_f.at[pl.ds(HALO, 14)], rows_recv.at[PLACES])
+        wait_bytes(tall_f.at[pl.ds(HALO, 2)], here_sem.at[2])
+        send_halo(tall_f, 1)
 
     @pl.when(points)
     def _():
@@ -483,7 +522,9 @@
 
     for row in range(2):
         added = f_rows[:, row].reshape(LOCAL, W).astype(F32) + branch_rows[row].astype(F32)
-        out_ref[row] = added.astype(BF16)
+        out_rows[row] = added.astype(BF16)
+    store_out = pltpu.make_async_copy(out_rows, out_hbm, here_sem.at[6])
+    store_out.start()
 
     @pl.when(works)
     def _():
@@ -492,7 +533,7 @@
         squares = jnp.sum(grads * grads, axis=1, keepdims=True) / (2 * K)
         steps = STEP_SIZE * grads * lax.rsqrt(squares + EPSILON)
         update[...] = steps
-        updates[place] = steps
+        pltpu.make_async_copy(update, updates.at[place], here_sem.at[7]).start()
 
         @loop(PLACES)
         def _(i):
@@ -513,7 +554,7 @@
     def _():
         wait_bytes(updates.at[pl.ds(0, GROUPS)], all_recv)
 
-    up_ref[...] = updates[...].reshape(W, W).T
+    store_out.wait()
 
     @pl.when(works)
     def _():
@@ -536,6 +577,7 @@
 
         wait_bytes(partials.at[pl.ds(0, LEVELS - 1)], sum_send)
         wait_bytes(updates.at[pl.ds(0, PLACES - 1)], all_send)
+        wait_bytes(update, here_sem.at[7])
 
     @pl.when(idles)
     def _():
@@ -561,10 +603,11 @@
 ):
     for row in range(2):
         out_ref[:, row, :] = out_rows[row]
-    new = h_ref[...] - step_ref[64 : 64 + K, 0:LOCAL]
+    steps = step_ref[...].reshape(W, W).T
+    new = h_ref[...] - steps[64 : 64 + K, 0:LOCAL]
     h_new[...] = new
     h_swa[...] = (AVERAGED * h_avg[...] + new) / (AVERAGED + 1)
-    new = v_ref[...] - step_ref[0:K, 0:LOCAL]
+    new = v_ref[...] - steps[0:K, 0:LOCAL]
     v_new[...] = new
     v_swa[...] = (AVERAGED * v_avg[...] + new) / (AVERAGED + 1)
 
@@ -589,11 +632,16 @@
         name="swa_step",
         out_shape=(
             jax.ShapeDtypeStruct((2, LOCAL, W), BF16),
-            jax.ShapeDtypeStruct((W, W), F32),
+            jax.ShapeDtypeStruct((PLACES, GROUP, W), F32),
         ),
-        in_specs=[hbm] * 2 + [vmem] * 4 + [hbm] * 2,
-        out_specs=(vmem, vmem),
+        in_specs=[hbm] * 8,
+        out_specs=(hbm, hbm),
         scratch_shapes=[
+            pltpu.VMEM((2, W), jnp.int32),
+            pltpu.VMEM((K, LOCAL), F32),
+            pltpu.VMEM((K, LOCAL), F32),
+            pltpu.VMEM((C // W, W), F32),
+            pltpu.VMEM((2, LOCAL, W), BF16),
             pltpu.VMEM((LOCAL, 2, W), BF16),
             pltpu.VMEM((LOCAL, 2, W), BF16),
             pltpu.VMEM((GROUPS, 2, GROUP, W), BF16),
@@ -627,12 +675,11 @@
             pltpu.VMEM((GROUP, W), BF16),
             pltpu.VMEM((LEVELS, GROUP, W), BF16),
             pltpu.VMEM((GROUP, W), F32),
-            pltpu.VMEM((PLACES, GROUP, W), F32),
-            pltpu.SemaphoreType.REGULAR((2,)),
-            dma((4,)),
-            dma((6,)),
+            pltpu.SemaphoreType.REGULAR((3,)),
+            dma((8,)),
+            dma((8,)),
             dma((2,)),
-            dma((2,)),
+            dma((PLACES + 1,)),
             dma((2, 4)),
             dma((2, 4)),
             dma,

time: 55.8 us -> 48.3 us (0.87)
  Pallas kernels: 54.9 us -> 47.5 us
    pallas_call x1, Pallas kernels: 53.3 us -> 45.9 us  [local(): pl.pallas_call(kernel, name='swa_step', out_shape=(jax.ShapeDtypeStruct((...]
where the time goes in v3:
time: 48.3 us; the launch traced here: 48.2 us
  Pallas kernels  47.5 us (98%)
  between operations  0.64 us (1%)
    pallas_call x1, Pallas kernels, local(): pl.pallas_call(kernel, name='swa_step', out_shape=(jax.ShapeDtypeStruct((...  45.9 us
    pallas_call x1, Pallas kernels, local(): pl.pallas_call(finish, name='finish', out_shape=(jax.ShapeDtypeStruct((LO...  1.65 us

profile of v3, /device:TPU:1, one launch (start us, length us, event | category | flops | bytes accessed | tf_op | source)
XLA Modules:
  0.0 48.2 jit_solution(14286780426884675834)
XLA Ops:
  0.6 45.9 %swa_step.1 = (bf16[2,96,128]{2,1,0:T(8,128)(2,1)}, f32[8,16,128]{2,1,0:T(8,128)}) custom-call(bf16[96,2,128]{2,1,0:T(2,128)(2,1)} %f_hbm.1, bf16[96,2,128]{2,1,0:T(2,128)(2,1)} %cot_hbm.1, s32[2,128]{1,0:T(2,128)} %tissue_hbm.1, f32[47,96]{1,0:T(8,128)} %bitcast.9, f32[47,96]{1,0:T(8,128)} %bitcast.11, f32[3,128]{1,0:T(4,128)} %bitcast.15, ...), custom_call_target="tpu_custom_call" | custom-call | tf_op jit(solution)/shard_map/swa_step/pallas_call | solution.py:630
  46.5 1.6 %finish.1 = (bf16[96,2,128]{2,1,0:T(2,128)(2,1)}, f32[47,96]{1,0:T(8,128)}, f32[47,96]{1,0:T(8,128)}, f32[47,96]{1,0:T(8,128)}, f32[47,96]{1,0:T(8,128)}) custom-call(bf16[2,96,128]{2,1,0:T(8,128)(2,1)} %get-tuple-element.12.out_rows, f32[8,16,128]{2,1,0:T(8,128)} %get-tuple-element.13.step_ref, f32[47,96]{1,0:T(8,128)} %bitcast.10, f32[47,96]{1,0:T(8,128)} %bitcast.12, ...), custom_call_target="tpu_custom_call" | custom-call | tf_op jit(solution)/shard_map/finish/pallas_call | solution.py:710

commit v4 on v3

--- a/solution.py
+++ b/solution.py
@@ -64,13 +64,13 @@
     w_out_t,
     gain,
     taps,
+    pads,
     smoothed,
     tall_s,
     tall_f,
     wide_s,
-    wide_f,
-    v_taps,
-    shifted,
+    matrix,
+    masked,
     mixed,
     cell_grads,
     grad_act,
@@ -141,26 +141,6 @@
     def loop(count):
         return lambda body: [body(i) for i in range(count)]
 
-    barrier = pltpu.get_barrier_semaphore()
-
-    for step in range(1, PLACES):
-        line = level + lax.rem(place + step, PLACES)
-        pl.semaphore_signal(barrier, 1, device_id=(line, y), device_id_type=MESH)
-    others = [lax.rem(y + step, COUNT_Y) for step in range(1, COUNT_Y)]
-    for to_y in others:
-        pl.semaphore_signal(barrier, 1, device_id=(band, to_y), device_id_type=MESH)
-
-    def tell(sem, step):
-        there = lax.rem(z + step + LEVELS, LEVELS)
-        pl.semaphore_signal(
-            sem, 1, device_id=(there * PLACES + place, y), device_id_type=MESH
-        )
-
-    @pl.when(works)
-    def _():
-        for step in (1, -1, 2, -2):
-            tell(barrier, step)
-
     load_in = pltpu.make_async_copy(w_in_hbm, w_in, load_sem.at[0])
     load_out = pltpu.make_async_copy(w_out_hbm, w_out, load_sem.at[1])
     load_f = pltpu.make_async_copy(f_hbm, f_pairs, load_sem.at[2])
@@ -174,36 +154,42 @@
     for load in (load_f, *small, load_cot, load_in, load_out):
         load.start()
 
-    for load in small:
-        load.wait()
-    taps[...] = jnp.zeros((2, W, W), F32)
-    taps[0, 0:K, 0:LOCAL] = h_ref[...]
-    taps[1, 0:K, 0:LOCAL] = v_ref[...]
-    h_half = taps[0].T[0:LOCAL].astype(BF16).astype(F32)
-    taps[1] = taps[1].T.astype(BF16).astype(F32)
-    column = lax.broadcasted_iota(jnp.int32, (LOCAL, W), 1)
+    barrier = pltpu.get_barrier_semaphore()
+
+    for step in range(1, PLACES):
+        line = level + lax.rem(place + step, PLACES)
+        pl.semaphore_signal(barrier, 1, device_id=(line, y), device_id_type=MESH)
+    others = [lax.rem(y + step, COUNT_Y) for step in range(1, COUNT_Y)]
+    for to_y in others:
+        pl.semaphore_signal(barrier, 1, device_id=(band, to_y), device_id_type=MESH)
+
+    def tell(sem, step):
+        there = lax.rem(z + step + LEVELS, LEVELS)
+        pl.semaphore_signal(
+            sem, 1, device_id=(there * PLACES + place, y), device_id_type=MESH
+        )
+
+    @pl.when(works)
+    def _():
+        for step in (1, -1, 2, -2):
+            tell(barrier, step)
+
+    pads[:, 0:HALO] = jnp.zeros((2, HALO, W), F32)
+    pads[:, HALO + W :] = jnp.zeros((2, HALO, W), F32)
+    small[0].wait()
+    h_ref[...] = h_ref[...].astype(BF16).astype(F32)
     load_f.wait()
-    sources = [f_pairs[:, row, :].astype(F32) for row in range(2)]
     for row in range(2):
-        f_rows[:, row] = sources[row].astype(BF16).reshape(GROUPS, GROUP, W)
-    sums = [jnp.zeros((LOCAL, W), F32) for row in range(2)]
+        source = f_pairs[:, row, :].astype(F32)
+        f_rows[:, row] = source.astype(BF16).reshape(GROUPS, GROUP, W)
+        pads[row, HALO : HALO + W, 0:LOCAL] = source.T
+    sums = [jnp.zeros((W, LOCAL), F32) for row in range(2)]
     for t in range(K):
-        weight = jnp.broadcast_to(h_half[:, t : t + 1], (LOCAL, W))
-        if t < RADIUS:
-            weight = jnp.where(column >= RADIUS - t, weight, 0.0)
-        if t > RADIUS:
-            weight = jnp.where(column < W + RADIUS - t, weight, 0.0)
+        weight = h_ref[t : t + 1, :]
         for row in range(2):
-            moved = sources[row]
-            if t != RADIUS:
-                moved = pltpu.roll(moved, (RADIUS - t) % W, 1)
-            sums[row] = sums[row] + weight * moved
+            sums[row] = sums[row] + weight * pads[row, t + 1 : t + 1 + W, 0:LOCAL]
     for row in range(2):
-        smoothed[:, row] = sums[row].astype(BF16).reshape(GROUPS, GROUP, W)
-    load_cot.wait()
-    for row in range(2):
-        mask = tissue_ref[row : row + 1, :].astype(F32)
-        w_rows[row] = (cot_pairs[:, row, :].astype(F32) * mask).astype(BF16)
+        smoothed[:, row] = sums[row].T.astype(BF16).reshape(GROUPS, GROUP, W)
 
     @pl.when(works)
     def _():
@@ -233,6 +219,12 @@
             y,
         )
 
+    for load in small[1:]:
+        load.wait()
+    load_cot.wait()
+    for row in range(2):
+        mask = tissue_ref[row : row + 1, :].astype(F32)
+        w_rows[row] = (cot_pairs[:, row, :].astype(F32) * mask).astype(BF16)
     for row in range(2):
         go(
             jnp.logical_and(points, y % 2 == row),
@@ -295,9 +287,6 @@
 
     @pl.when(works)
     def _():
-        v_half = taps[1, pl.ds(pl.multiple_of(place * GROUP, GROUP), GROUP), :]
-        for t in range(K):
-            v_taps[t] = jnp.broadcast_to(v_half[:, t : t + 1], (GROUP, W))
         for hop, flip in ((0, 0), (0, 1), (1, 0), (1, 1), (3, 0), (3, 1), (2, 0), (2, 1)):
             source = lax.rem(place + 2 * hop, PLACES)
             if flip:
@@ -328,6 +317,20 @@
                         y,
                     ).start()
 
+        taps[...] = jnp.zeros((W, W), F32)
+        taps[0:K, 0:LOCAL] = v_ref[...]
+        taps[...] = taps[...].T
+        v_half = taps[pl.ds(pl.multiple_of(place * GROUP, GROUP), GROUP), :].astype(BF16)
+        wide_lane = lax.broadcasted_iota(jnp.int32, (W, TALL * GROUP), 1)
+        wide_tap = lax.broadcasted_iota(jnp.int32, (W, TALL * GROUP), 0)
+        spread = (wide_lane // GROUP == wide_tap).astype(F32).astype(BF16)
+        base = jnp.dot(v_half, spread, preferred_element_type=F32)
+        group_lane = lax.broadcasted_iota(jnp.int32, (GROUP, TALL * GROUP), 1)
+        group_row = lax.broadcasted_iota(jnp.int32, (GROUP, TALL * GROUP), 0)
+        base = jnp.where(group_lane % GROUP == group_row, base, 0.0)
+        for r in range(ROWS):
+            moved = pltpu.roll(base, GROUP * (r + 1), 1)
+            matrix[r * GROUP : (r + 1) * GROUP] = moved.astype(BF16)
 
     load_in.wait()
     load_out.wait()
@@ -354,20 +357,14 @@
             grad_act[at, :] = jnp.dot(w_out[at, :], upstream, preferred_element_type=F32)
 
 
-    def row_convolution(wide):
-        def tap(t, acc):
-            return acc + v_taps[t][None] * wide[pl.ds(t + 1, ROWS)]
-
-        acc = jnp.zeros((ROWS, GROUP, W), F32)
-        for t in range(K):
-            acc = tap(t, acc)
-        return acc
+    def row_convolution(tall):
+        flat = tall[...].reshape(TALL * GROUP, W)
+        return jnp.dot(matrix[...], flat, preferred_element_type=F32)
 
     @pl.when(works)
     def _():
         wait_halo(tall_s, 0)
-        wide_s[...] = tall_s[...].astype(F32)
-        mixed[...] = row_convolution(wide_s).astype(BF16)
+        mixed[...] = row_convolution(tall_s).astype(BF16).reshape(ROWS, GROUP, W)
 
         @loop(ROWS)
         def _(r):
@@ -461,18 +458,18 @@
         tell(far_sem.at[1], 4)
         tell(far_sem.at[1], -4)
         wait_halo(tall_f, 1)
-        wide_f[...] = tall_f[...].astype(F32)
-        rows_f = row_convolution(wide_f)
-        column = lax.broadcasted_iota(jnp.int32, (ROWS * GROUP, W), 1)
-        rows_f = rows_f.reshape(ROWS * GROUP, W)
-
-        @loop(K)
-        def _(t):
-            moved = pltpu.roll(rows_f, lax.rem(W + RADIUS - t, W), 1)
-            first = column + (t - RADIUS)
-            moved = jnp.where(jnp.logical_and(first >= 0, first < W), moved, 0.0)
-            shifted[t] = moved.reshape(ROWS, GROUP, W)
-
+        wide_s[...] = tall_s[...].astype(F32)
+        rows_f = row_convolution(tall_f).astype(BF16)
+        first = lax.broadcasted_iota(jnp.int32, (W, W), 0)
+        second = lax.broadcasted_iota(jnp.int32, (W, W), 1)
+        mirror = (first + second == W - 1).astype(F32).astype(BF16)
+        turned = lax.dot_general(
+            mirror, rows_f, (((1,), (1,)), ((), ())), preferred_element_type=F32
+        )
+        channel = lax.broadcasted_iota(jnp.int32, (W, ROWS * GROUP), 1) % GROUP
+        for c in range(GROUP):
+            kept = jnp.where(channel == c, turned, 0.0)
+            masked[c * W : (c + 1) * W] = kept.astype(BF16)
         @pl.when(points)
         def _():
             wait_bytes(grad_rows.at[pl.ds(0, ROWS - 1)], back_recv)
@@ -482,17 +479,21 @@
         def _():
             wait_bytes(grad_rows, back_recv)
 
+        flat = grad_rows[...].reshape(ROWS * GROUP, W)
+        near = jnp.abs(first + second - (W - 1)) <= RADIUS
+        h_sums = []
+        for part in range(4):
+            at = pl.ds(part * 4 * W, 4 * W)
+            pairs = jnp.dot(masked[at, :], flat, preferred_element_type=F32)
+            for c in range(4):
+                block = jnp.where(near, pairs[c * W : (c + 1) * W], 0.0)
+                block = pltpu.roll(block, 0, 1, stride=1, stride_axis=0)
+                h_sums.append(jnp.sum(block, axis=0, keepdims=True))
+        sums = jnp.concatenate(h_sums, axis=0)
         grads = grad_rows[...].astype(F32)
-
-        def tap(t, sums):
+        for t in range(K):
             v_sum = jnp.sum(grads * wide_s[pl.ds(t + 1, ROWS)], axis=0)
-            h_sum = jnp.sum(grads * shifted[t], axis=0)
-            sums = jnp.where(lane == t, jnp.sum(v_sum, axis=1, keepdims=True), sums)
-            return jnp.where(lane == t + 64, jnp.sum(h_sum, axis=1, keepdims=True), sums)
-
-        sums = jnp.zeros((GROUP, W), F32)
-        for t in range(K):
-            sums = tap(t, sums)
+            sums = jnp.where(lane == t + 32, jnp.sum(v_sum, axis=1, keepdims=True), sums)
         partial[...] = sums.astype(BF16)
         partials[z] = sums.astype(BF16)
         pl.semaphore_wait(far_sem.at[1], 2)
@@ -532,7 +533,7 @@
         grads = jnp.sum(partials[...].astype(F32), axis=0)
         squares = jnp.sum(grads * grads, axis=1, keepdims=True) / (2 * K)
         steps = STEP_SIZE * grads * lax.rsqrt(squares + EPSILON)
-        update[...] = steps
+        update[...] = steps.astype(BF16)
         pltpu.make_async_copy(update, updates.at[place], here_sem.at[7]).start()
 
         @loop(PLACES)
@@ -603,7 +604,17 @@
 ):
     for row in range(2):
         out_ref[:, row, :] = out_rows[row]
-    steps = step_ref[...].reshape(W, W).T
+    row = lax.broadcasted_iota(jnp.int32, (W, W), 0)
+    lane = lax.broadcasted_iota(jnp.int32, (W, W), 1)
+    from_v = jnp.logical_and(row < K, lane == row + 32)
+    from_h = jnp.logical_and(row >= 64, lane == (214 - row) % W)
+    order = jnp.logical_or(from_v, from_h).astype(F32).astype(BF16)
+    steps = lax.dot_general(
+        order,
+        step_ref[...].reshape(W, W),
+        (((1,), (1,)), ((), ())),
+        preferred_element_type=F32,
+    )
     new = h_ref[...] - steps[64 : 64 + K, 0:LOCAL]
     h_new[...] = new
     h_swa[...] = (AVERAGED * h_avg[...] + new) / (AVERAGED + 1)
@@ -632,7 +643,7 @@
         name="swa_step",
         out_shape=(
             jax.ShapeDtypeStruct((2, LOCAL, W), BF16),
-            jax.ShapeDtypeStruct((PLACES, GROUP, W), F32),
+            jax.ShapeDtypeStruct((PLACES, GROUP, W), BF16),
         ),
         in_specs=[hbm] * 8,
         out_specs=(hbm, hbm),
@@ -651,14 +662,14 @@
             pltpu.VMEM((HID, C), BF16),
             pltpu.VMEM((C, HID), BF16),
             pltpu.VMEM((C, W), F32),
-            pltpu.VMEM((2, W, W), F32),
+            pltpu.VMEM((W, W), F32),
+            pltpu.VMEM((2, W + 2 * HALO, W), F32),
             pltpu.VMEM((GROUPS, 2, GROUP, W), BF16),
             pltpu.VMEM((TALL, GROUP, W), BF16),
             pltpu.VMEM((TALL, GROUP, W), BF16),
             pltpu.VMEM((TALL, GROUP, W), F32),
-            pltpu.VMEM((TALL, GROUP, W), F32),
-            pltpu.VMEM((K, GROUP, W), F32),
-            pltpu.VMEM((K, ROWS, GROUP, W), F32),
+            pltpu.VMEM((ROWS * GROUP, TALL * GROUP), BF16),
+            pltpu.VMEM((GROUP * W, ROWS * GROUP), BF16),
             pltpu.VMEM((ROWS, GROUP, W), BF16),
             pltpu.VMEM((COUNT_Y, LOCAL, W), BF16),
             pltpu.VMEM((HID, W), F32),
@@ -674,7 +685,7 @@
             pltpu.VMEM((2, LOCAL, W), BF16),
             pltpu.VMEM((GROUP, W), BF16),
             pltpu.VMEM((LEVELS, GROUP, W), BF16),
-            pltpu.VMEM((GROUP, W), F32),
+            pltpu.VMEM((GROUP, W), BF16),
             pltpu.SemaphoreType.REGULAR((3,)),
             dma((8,)),
             dma((8,)),

time: 48.3 us -> 46.9 us (0.971)
  Pallas kernels: 47.5 us -> 46 us
    pallas_call x1, Pallas kernels: 45.9 us -> 44.4 us  [local(): pl.pallas_call(kernel, name='swa_step', out_shape=(jax.ShapeDtypeStruct((...]
where the time goes in v4:
time: 46.9 us; the launch traced here: 46.7 us
  Pallas kernels  46 us (98%)
  between operations  0.64 us (1%)
    pallas_call x1, Pallas kernels, local(): pl.pallas_call(kernel, name='swa_step', out_shape=(jax.ShapeDtypeStruct((...  44.4 us
    pallas_call x1, Pallas kernels, local(): pl.pallas_call(finish, name='finish', out_shape=(jax.ShapeDtypeStruct((LO...  1.67 us

profile of v4, /device:TPU:1, one launch (start us, length us, event | category | flops | bytes accessed | tf_op | source)
XLA Modules:
  0.0 46.7 jit_solution(11067180775057237641)
XLA Ops:
  0.6 44.4 %swa_step.1 = (bf16[2,96,128]{2,1,0:T(8,128)(2,1)}, bf16[8,16,128]{2,1,0:T(8,128)(2,1)}) custom-call(bf16[96,2,128]{2,1,0:T(2,128)(2,1)} %f_hbm.1, bf16[96,2,128]{2,1,0:T(2,128)(2,1)} %cot_hbm.1, s32[2,128]{1,0:T(2,128)} %tissue_hbm.1, f32[47,96]{1,0:T(8,128)} %bitcast.9, f32[47,96]{1,0:T(8,128)} %bitcast.11, f32[3,128]{1,0:T(4,128)} %bitcast.15, ...), custom_call_target="tpu_custom_call" | custom-call | tf_op jit(solution)/shard_map/swa_step/pallas_call | solution.py:641
  45.0 1.7 %finish.1 = (bf16[96,2,128]{2,1,0:T(2,128)(2,1)}, f32[47,96]{1,0:T(8,128)}, f32[47,96]{1,0:T(8,128)}, f32[47,96]{1,0:T(8,128)}, f32[47,96]{1,0:T(8,128)}) custom-call(bf16[2,96,128]{2,1,0:T(8,128)(2,1)} %get-tuple-element.12.out_rows, bf16[8,16,128]{2,1,0:T(8,128)(2,1)} %get-tuple-element.13.step_ref, f32[47,96]{1,0:T(8,128)} %bitcast.10, ...), custom_call_target="tpu_custom_call" | custom-call | tf_op jit(solution)/shard_map/finish/pallas_call | solution.py:721

commit v5 on v4

--- a/solution.py
+++ b/solution.py
@@ -71,6 +71,7 @@
     wide_s,
     matrix,
     masked,
+    v_sums,
     mixed,
     cell_grads,
     grad_act,
@@ -427,7 +428,7 @@
                 grad_cells.at[i],
                 grad_rows.at[my_row],
                 back_send,
-                back_recv,
+                back_recv.at[place // 2],
                 here_sem.at[4],
                 level + to_place,
                 to_y,
@@ -470,14 +471,30 @@
         for c in range(GROUP):
             kept = jnp.where(channel == c, turned, 0.0)
             masked[c * W : (c + 1) * W] = kept.astype(BF16)
-        @pl.when(points)
-        def _():
-            wait_bytes(grad_rows.at[pl.ds(0, ROWS - 1)], back_recv)
-            wait_bytes(grad_rows.at[0], here_sem.at[4])
-
-        @pl.when(rests)
-        def _():
-            wait_bytes(grad_rows, back_recv)
+        def v_part(group, t):
+            rows = grad_rows[pl.ds(4 * group, 4)].astype(F32)
+            return jnp.sum(rows * wide_s[pl.ds(4 * group + t + 1, 4)], axis=0)
+
+        for nth, offset in enumerate((0, 1, 3)):
+            group = lax.rem(place // 2 + offset, 4)
+            if offset == 0:
+
+                @pl.when(points)
+                def _(group=group):
+                    wait_bytes(grad_rows.at[pl.ds(0, 3)], back_recv.at[group])
+                    wait_bytes(grad_rows.at[0], here_sem.at[4])
+
+                @pl.when(rests)
+                def _(group=group):
+                    wait_bytes(grad_rows.at[pl.ds(0, 4)], back_recv.at[group])
+
+            else:
+                wait_bytes(grad_rows.at[pl.ds(0, 4)], back_recv.at[group])
+            for t in range(K):
+                part = v_part(group, t)
+                v_sums[t] = v_sums[t] + part if nth else part
+        group = lax.rem(place // 2 + 2, 4)
+        wait_bytes(grad_rows.at[pl.ds(0, 4)], back_recv.at[group])
 
         flat = grad_rows[...].reshape(ROWS * GROUP, W)
         near = jnp.abs(first + second - (W - 1)) <= RADIUS
@@ -490,9 +507,8 @@
                 block = pltpu.roll(block, 0, 1, stride=1, stride_axis=0)
                 h_sums.append(jnp.sum(block, axis=0, keepdims=True))
         sums = jnp.concatenate(h_sums, axis=0)
-        grads = grad_rows[...].astype(F32)
         for t in range(K):
-            v_sum = jnp.sum(grads * wide_s[pl.ds(t + 1, ROWS)], axis=0)
+            v_sum = v_sums[t] + v_part(group, t)
             sums = jnp.where(lane == t + 32, jnp.sum(v_sum, axis=1, keepdims=True), sums)
         partial[...] = sums.astype(BF16)
         partials[z] = sums.astype(BF16)
@@ -527,6 +543,46 @@
     store_out = pltpu.make_async_copy(out_rows, out_hbm, here_sem.at[6])
     store_out.start()
 
+    store_out.wait()
+
+    @pl.when(works)
+    def _():
+        for which, tall in enumerate((tall_s, tall_f)):
+            wait_bytes(tall.at[pl.ds(0, 10)], rows_send.at[which])
+            for m, (step, here, there, rows) in enumerate(moves):
+
+                @pl.when(inside(step))
+                def _(m=m, tall=tall, which=which, here=here, rows=rows):
+                    wait_bytes(tall.at[pl.ds(here, rows)], halo_send.at[which, m])
+
+        @pl.when(points)
+        def _():
+            wait_bytes(mixed.at[pl.ds(0, ROWS - 1)], mix_send)
+            wait_bytes(grad_cells.at[pl.ds(0, C // GROUP - 1)], back_send)
+
+        @pl.when(rests)
+        def _():
+            wait_bytes(mixed, mix_send)
+
+
+    @pl.when(idles)
+    def _():
+        for which, tall in enumerate((tall_s, tall_f)):
+            wait_bytes(tall.at[pl.ds(0, 12)], rows_send.at[which])
+
+        @pl.when(points)
+        def _():
+            wait_bytes(grad_cells, back_send)
+
+    @pl.when(points)
+    def _():
+        wait_bytes(cell_grads.at[0], cot_send)
+        wait_bytes(branch_cells.at[pl.ds(0, COUNT_Y - 1)], branch_send)
+
+    @pl.when(rests)
+    def _():
+        wait_bytes(cell_grads.at[pl.ds(0, 2)], cot_send)
+
     @pl.when(works)
     def _():
         wait_bytes(partials.at[pl.ds(0, LEVELS - 1)], sum_recv)
@@ -549,54 +605,14 @@
                     y,
                 ).start()
 
+        wait_bytes(partials.at[pl.ds(0, LEVELS - 1)], sum_send)
+        wait_bytes(update, here_sem.at[7])
+        wait_bytes(updates.at[pl.ds(0, PLACES - 1)], all_send)
         wait_bytes(updates.at[pl.ds(0, GROUPS - 1)], all_recv)
 
     @pl.when(idles)
     def _():
         wait_bytes(updates.at[pl.ds(0, GROUPS)], all_recv)
-
-    store_out.wait()
-
-    @pl.when(works)
-    def _():
-        for which, tall in enumerate((tall_s, tall_f)):
-            wait_bytes(tall.at[pl.ds(0, 10)], rows_send.at[which])
-            for m, (step, here, there, rows) in enumerate(moves):
-
-                @pl.when(inside(step))
-                def _(m=m, tall=tall, which=which, here=here, rows=rows):
-                    wait_bytes(tall.at[pl.ds(here, rows)], halo_send.at[which, m])
-
-        @pl.when(points)
-        def _():
-            wait_bytes(mixed.at[pl.ds(0, ROWS - 1)], mix_send)
-            wait_bytes(grad_cells.at[pl.ds(0, C // GROUP - 1)], back_send)
-
-        @pl.when(rests)
-        def _():
-            wait_bytes(mixed, mix_send)
-
-        wait_bytes(partials.at[pl.ds(0, LEVELS - 1)], sum_send)
-        wait_bytes(updates.at[pl.ds(0, PLACES - 1)], all_send)
-        wait_bytes(update, here_sem.at[7])
-
-    @pl.when(idles)
-    def _():
-        for which, tall in enumerate((tall_s, tall_f)):
-            wait_bytes(tall.at[pl.ds(0, 12)], rows_send.at[which])
-
-        @pl.when(points)
-        def _():
-            wait_bytes(grad_cells, back_send)
-
-    @pl.when(points)
-    def _():
-        wait_bytes(cell_grads.at[0], cot_send)
-        wait_bytes(branch_cells.at[pl.ds(0, COUNT_Y - 1)], branch_send)
-
-    @pl.when(rests)
-    def _():
-        wait_bytes(cell_grads.at[pl.ds(0, 2)], cot_send)
 
 
 def finish(
@@ -670,6 +686,7 @@
             pltpu.VMEM((TALL, GROUP, W), F32),
             pltpu.VMEM((ROWS * GROUP, TALL * GROUP), BF16),
             pltpu.VMEM((GROUP * W, ROWS * GROUP), BF16),
+            pltpu.VMEM((K, GROUP, W), F32),
             pltpu.VMEM((ROWS, GROUP, W), BF16),
             pltpu.VMEM((COUNT_Y, LOCAL, W), BF16),
             pltpu.VMEM((HID, W), F32),
@@ -698,7 +715,7 @@
             dma,
             dma,
             dma,
-            dma,
+            dma((4,)),
             dma,
             dma,
             dma,

time: 46.9 us -> 46.6 us (level)
  no operation moved by 1% of the time
where the time goes in v5:
time: 46.6 us; the launch traced here: 46.5 us
  Pallas kernels  45.8 us (98%)
  between operations  0.64 us (1%)
    pallas_call x1, Pallas kernels, local(): pl.pallas_call(kernel, name='swa_step', out_shape=(jax.ShapeDtypeStruct((...  44.1 us
    pallas_call x1, Pallas kernels, local(): pl.pallas_call(finish, name='finish', out_shape=(jax.ShapeDtypeStruct((LO...  1.67 us

profile of v5, /device:TPU:1, one launch (start us, length us, event | category | flops | bytes accessed | tf_op | source)
XLA Modules:
  0.0 46.5 jit_solution(12630288669112733826)
XLA Ops:
  0.6 44.1 %swa_step.1 = (bf16[2,96,128]{2,1,0:T(8,128)(2,1)}, bf16[8,16,128]{2,1,0:T(8,128)(2,1)}) custom-call(bf16[96,2,128]{2,1,0:T(2,128)(2,1)} %f_hbm.1, bf16[96,2,128]{2,1,0:T(2,128)(2,1)} %cot_hbm.1, s32[2,128]{1,0:T(2,128)} %tissue_hbm.1, f32[47,96]{1,0:T(8,128)} %bitcast.9, f32[47,96]{1,0:T(8,128)} %bitcast.11, f32[3,128]{1,0:T(4,128)} %bitcast.15, ...), custom_call_target="tpu_custom_call" | custom-call | tf_op jit(solution)/shard_map/swa_step/pallas_call | solution.py:657
  44.8 1.7 %finish.1 = (bf16[96,2,128]{2,1,0:T(2,128)(2,1)}, f32[47,96]{1,0:T(8,128)}, f32[47,96]{1,0:T(8,128)}, f32[47,96]{1,0:T(8,128)}, f32[47,96]{1,0:T(8,128)}) custom-call(bf16[2,96,128]{2,1,0:T(8,128)(2,1)} %get-tuple-element.12.out_rows, bf16[8,16,128]{2,1,0:T(8,128)(2,1)} %get-tuple-element.13.step_ref, f32[47,96]{1,0:T(8,128)} %bitcast.10, ...), custom_call_target="tpu_custom_call" | custom-call | tf_op jit(solution)/shard_map/finish/pallas_call | solution.py:738
